TPU v7x, 32 devices: a whole 2x2x4 slice. The times are simulated.
32 devices in a mesh: node: 8 (over y, x, core), local: 4 (over z).
Axes of the slice: x: 2, y: 2, z: 4, core: 2. Of those that a mesh axis runs over, the one named last changes fastest.
Arguments:
- tokens: bfloat16 [8192, 8192], P(('node', 'local')), may hold values from -6 to 6
- grad_hidden: bfloat16 [8192, 256], P(('node', 'local')), may hold values from -0.0625 to 0.0625
- gate_pre: bfloat16 [8192, 256], P(('node', 'local')), may hold values from -6 to 6
- momentum: float32 [8192, 256], P('local'), may hold values from -6 to 6
Outputs:
- momentum_new: float32 [8192, 256], P('local')
All inputs are finite; a program needn't handle non-finite values.
Results may differ from a plain program's by a relative error of at most 0.012.
Values may be sent and summed in bfloat16 or wider, within the bound.
No kernel may reach another device: no remote copies, remote signals or barrier semaphores. Data moves between devices by JAX's collectives and lax.ppermute only.
A program may use at most 64 MiB of HBM per device.

v0:
```python
import jax
import jax.numpy as jnp
from jax import lax
from jax.sharding import PartitionSpec as P


def per_device(tokens, grad_hidden, gate_pre, momentum):
    up_grad = (grad_hidden.astype(jnp.float32) * jax.nn.silu(gate_pre.astype(jnp.float32))).astype(
        jnp.bfloat16
    )
    owned_rows = momentum.shape[0]
    columns = up_grad.shape[1]
    node_total = lax.psum_scatter(
        lax.dot_general(
            tokens, up_grad, (((0,), (0,)), ((), ())), preferred_element_type=jnp.float32
        ).astype(jnp.bfloat16),
        "local",
        scatter_dimension=0,
        tiled=True,
    )
    nodes = lax.axis_size("node")
    span = owned_rows // nodes
    reduced = jnp.sum(
        lax.all_to_all(
            node_total.reshape(nodes, span, columns),
            "node",
            split_axis=0,
            concat_axis=0,
            tiled=True,
        ).astype(jnp.float32),
        axis=0,
    )
    shard = reduced.astype(jnp.bfloat16)
    gathered = lax.all_gather(shard, "node", axis=0, tiled=True)
    return 0.9 * momentum + gathered.astype(jnp.float32)


def solution(mesh):
    in_specs = (
        P(("node", "local"), None),
        P(("node", "local"), None),
        P(("node", "local"), None),
        P("local", None),
    )
    out_specs = P("local", None)
    return jax.shard_map(
        per_device, mesh=mesh, in_specs=in_specs, out_specs=out_specs, check_vma=False
    )
```

profile of v0, /device:TPU:0, one launch (start us, length us, event | category | flops | bytes accessed | tf_op | source)
XLA Modules:
  0.0 147.6 jit_solution(13718607606032897228)
XLA Ops:
  6.5 0.0 reduce-scatter.2.cloned.1.call-start
  6.5 5.6 %fusion = bf16[8192,256]{0,1:T(8,128)(2,1)} fusion(bf16[256,8192]{1,0:T(8,128)(2,1)} %param.4, bf16[256,256]{1,0:T(8,128)(2,1)} %param.6, bf16[256,256]{1,0:T(8,128)(2,1)} %param.5), kind=kOutput, calls=%fused_computation.1 | convolution fusion | flops 1076363264 | bytes 8650752 | tf_op jit(solution)/shard_map/dot_general | solution.py:14
  12.1 0.0 reduce-scatter.2.cloned.1.call-update
  12.2 0.0 all-gather.2.cloned.1.call-start
  12.2 79.6 %reduce-scatter.2.cloned.1.call-done = bf16[2048,256]{0,1:T(8,128)(2,1)} async-done(((bf16[8192,256]{0,1:T(8,128)(2,1)}), bf16[2048,256]{0,1:T(8,128)(2,1)}) %reduce-scatter.2.cloned.1.call-update) | async-done | bytes 1048592 | tf_op jit(solution)/shard_map/reduce_scatter | solution.py:13
  91.8 1.3 copy.12
  93.1 18.8 %all_to_all.5 = bf16[8,256,256]{1,2,0:T(8,128)(2,1)S(1)} all-to-all(bf16[8,256,256]{1,2,0:T(8,128)(2,1)S(1)} %bitcast.7), channel_id=1, replica_groups=mesh['node'=8,'local'=4] {'node'}, dimensions={0} | all-to-all | bytes 2097152 | tf_op jit(solution)/shard_map/all_to_all | solution.py:24
  111.9 0.8 reduce_sum.12
  112.7 0.0 all-gather.2.cloned.1.call-update
  112.8 1.9 %copy.5 = f32[2048,256]{0,1:T(8,128)S(1)} copy(f32[2048,256]{1,0:T(8,128)} %param.7) | data formatting | bytes 4194304 | tf_op args[3]
  114.7 20.4 %all-gather.2.cloned.1.call-done = bf16[2048,256]{0,1:T(8,128)(2,1)} async-done(((bf16[256,256]{0,1:T(8,128)(2,1)}), bf16[2048,256]{0,1:T(8,128)(2,1)}) %all-gather.2.cloned.1.call-update) | async-done | bytes 1048592 | tf_op jit(solution)/shard_map/all_gather | solution.py:34
  135.1 2.9 %convert_add_fusion = f32[2048,256]{0,1:T(8,128)} fusion(bf16[2048,256]{0,1:T(8,128)(2,1)} %all-gather.2.cloned.1.call-done, f32[2048,256]{0,1:T(8,128)S(1)} %copy.5), kind=kLoop, calls=%fused_computation.2 | loop fusion | flops 1572864 | bytes 5242880 | tf_op jit(solution)/shard_map/add | solution.py:35
  137.9 2.9 %copy.8 = f32[2048,256]{1,0:T(8,128)} copy(f32[2048,256]{0,1:T(8,128)} %convert_add_fusion) | data formatting | bytes 4194304 | tf_op jit(solution)/shard_map/add | solution.py:35
Async XLA Ops:
  6.5 85.3 %reduce-scatter.2.cloned.1.call-start = ((), (), s32[]{:S(2)}) async-start(), calls=%async_computation.2 | async-start | bytes 5242880 | tf_op jit(solution)/shard_map/reduce_scatter | solution.py:13
  12.2 122.9 %all-gather.2.cloned.1.call-start = ((), (), s32[]{:S(2)}) async-start(), calls=%async_computation.3 | async-start | bytes 1179648 | tf_op jit(solution)/shard_map/all_gather | solution.py:34
Sparse Core Ops, SparseCore 0:
  12.3 79.5 reduce-scatter.1
  112.9 22.1 all-gather.1
where the time goes:
time: 148 us
  waiting for transfers between devices  100 us (68%)
  blocking collectives  18.8 us (13%)
  between operations  13.4 us (9%)
  local copies, waits for them, and re-layouts  6.1 us (4%)
  matrix products  5.59 us (4%)
  other arithmetic  3.67 us (2%)
    reduce_scatter x1, waiting for transfers between devices, per_device(): lax.psum_scatter(lax.dot_general(tokens, up_grad, (((0,), (0,)), ((), ())...  79.6 us
    all_gather x1, waiting for transfers between devices, per_device(): gathered = lax.all_gather(shard, 'node', axis=0, tiled=True)  20.4 us
    all_to_all x1, blocking collectives, per_device(): lax.all_to_all(node_total.reshape(nodes, span, columns), 'node', split_ax...  18.8 us
    dot_general x1, matrix products, per_device(): lax.dot_general(tokens, up_grad, (((0,), (0,)), ((), ())), preferred_elem...  5.59 us
  transfers between devices with their start and end apart: 2, of which 2 were waited for; matrix products, arithmetic and copies ran while one was open for 1% of the time, Pallas kernels for 0%

commit v1 on v0

--- a/solution.py
+++ b/solution.py
@@ -1,10 +1,250 @@
+import functools
+import math
+
 import jax
 import jax.numpy as jnp
 from jax import lax
+from jax.experimental import pallas as pl
+from jax.experimental.pallas import tpu as pltpu
 from jax.sharding import PartitionSpec as P
 
 
-def per_device(tokens, grad_hidden, gate_pre, momentum):
+ANY = pl.BlockSpec(memory_space=pl.ANY)
+HBM = pl.BlockSpec(memory_space=pltpu.HBM)
+VMEM = pl.BlockSpec(memory_space=pltpu.VMEM)
+PARAMS = pltpu.CompilerParams(vmem_limit_bytes=12 << 20)
+
+
+def near(x):
+    return pltpu.with_memory_space_constraint(x, pltpu.VMEM)
+
+
+def far_off(x):
+    return pltpu.with_memory_space_constraint(x, pltpu.HBM)
+
+
+def after(values, *others):
+    return lax.optimization_barrier((values, others))[0]
+
+
+def position(side):
+    n = lax.axis_index("node")
+    chip = lax.div(n, 2)
+    return lax.rem(n, 2), lax.rem(chip, side), lax.div(chip, side), lax.axis_index("local")
+
+
+def place(core, x, y, first, second, side):
+    ahead = lax.bitwise_xor(y, jnp.where(core == 0, second, first))
+    across = lax.bitwise_xor(x, jnp.where(core == 0, first, second))
+    return ahead * side + across
+
+
+def product_kernel(side, depth, other, groups, part, from_inputs, added, *refs):
+    refs = list(refs)
+    tokens = refs.pop(0)
+    if from_inputs:
+        grad, gate = refs.pop(0), refs.pop(0)
+    else:
+        left_ref = refs.pop(0)
+    addend = refs.pop(0) if added else None
+    outs = [refs.pop(0) for _ in groups]
+    if from_inputs:
+        left_ref = refs.pop(0)
+    held, sems = refs[:2]
+    core, x, y, z = position(side)
+    half = 1 - core if other else core
+    chips = side * side
+    block = tokens.shape[1] // (2 * chips * depth)
+    order = [(g, j, at) for g, group in enumerate(groups) for j, at in enumerate(group)]
+
+    copies = []
+    for i, (_, _, (f, s, q)) in enumerate(order):
+        row = (lax.bitwise_xor(z, q) * 2 + half) * chips + place(half, x, y, f, s, side)
+        start = pl.multiple_of(row * block, block)
+        copies.append(
+            pltpu.make_async_copy(tokens.at[:, pl.ds(start, block)], held.at[:, pl.ds(i * block, block)], sems.at[i])
+        )
+    if from_inputs:
+        small = [pltpu.make_async_copy(a, refs[2].at[i], refs[3].at[i]) for i, a in enumerate((grad, gate))]
+        for copy in small:
+            copy.start()
+    for copy in copies:
+        copy.start()
+    if from_inputs:
+        for copy in small:
+            copy.wait()
+        v = refs[2][1].astype(jnp.float32)
+        up = refs[2][0].astype(jnp.float32) * (v / (1.0 + jnp.exp(-v)))
+        left_ref[...] = up.astype(jnp.bfloat16).T
+    left = left_ref[part[0] : part[1], :]
+    for copy in copies:
+        copy.wait()
+    for i, (g, j, _) in enumerate(order):
+        value = jnp.dot(left, held[:, pl.ds(i * block, block)], preferred_element_type=jnp.float32)
+        if added:
+            value = value + addend[i].astype(jnp.float32)
+        outs[g][j] = value.astype(jnp.bfloat16)
+
+
+def products(tokens, ups, addend, other, groups, part, side, depth, block):
+    from_inputs = len(ups) == 2
+    token_rows, columns = ups[0].shape if from_inputs else ups[0].shape[::-1]
+    count = sum(len(group) for group in groups)
+    outs = [pltpu.VMEM((len(group), part[1] - part[0], block), jnp.bfloat16) for group in groups]
+    if from_inputs:
+        outs.append(pltpu.VMEM((columns, token_rows), jnp.bfloat16))
+        tokens, ups = far_off(tokens), [far_off(u) for u in ups]
+        extra = [pltpu.VMEM((2, *ups[0].shape), ups[0].dtype), pltpu.SemaphoreType.DMA((2,))]
+    else:
+        tokens, ups = near(tokens), [near(u) for u in ups]
+        extra = []
+    addends = [] if addend is None else [near(addend)]
+    return pl.pallas_call(
+        functools.partial(product_kernel, side, depth, other, groups, part, from_inputs, bool(addends)),
+        out_shape=outs,
+        in_specs=[HBM if from_inputs else VMEM] * (1 + len(ups)) + [VMEM] * len(addends),
+        out_specs=[VMEM] * len(outs),
+        scratch_shapes=[
+            pltpu.VMEM((token_rows, count * block), jnp.bfloat16),
+            pltpu.SemaphoreType.DMA((count,)),
+            *extra,
+        ],
+        compiler_params=PARAMS,
+        name="products",
+    )(tokens, *ups, *addends)
+
+
+def update_kernel(side, swapped, *refs):
+    chips = side * side
+    momentum, wide, *pieces = refs[: 2 + chips]
+    out, held, sems = refs[-3:]
+    core, x, y, _ = position(side)
+    block = momentum.shape[0] // (2 * chips)
+    c = 1 - core if swapped else core
+    copies = []
+    for i in range(chips):
+        start = (c * chips + place(c, x, y, i // side, i % side, side)) * block
+        rows = pl.ds(pl.multiple_of(start, block), block)
+        reduced = jnp.concatenate([wide[i], pieces[i][...]], axis=0)
+        held[i] = momentum[rows, :] + reduced.T.astype(jnp.float32)
+        copies.append(pltpu.make_async_copy(held.at[i], out.at[rows, :], sems.at[i]))
+        copies[-1].start()
+    for copy in copies:
+        copy.wait()
+
+
+def update(out, momentum, wide, pieces, swapped, side):
+    again = [] if out is None else [out]
+    rows, columns = momentum.shape
+    chips = len(pieces)
+    return pl.pallas_call(
+        functools.partial(update_kernel, side, swapped),
+        out_shape=jax.ShapeDtypeStruct(momentum.shape, momentum.dtype),
+        in_specs=[VMEM] * (2 + chips) + [HBM] * len(again),
+        out_specs=HBM,
+        input_output_aliases={2 + chips: 0} if again else {},
+        scratch_shapes=[
+            pltpu.VMEM((chips, rows // (2 * chips), columns), jnp.float32),
+            pltpu.SemaphoreType.DMA((chips,)),
+        ],
+        compiler_params=PARAMS,
+        name="update",
+    )(near(momentum), near(wide), *[near(p) for p in pieces], *again)
+
+
+def gathered_kernel(side, *refs):
+    *parts, out = refs
+    for i in range(len(parts)):
+        value = None
+        for k, part in enumerate(parts):
+            f, s = i // side ^ k // side, i % side ^ k % side
+            addend = part[f * side + s].astype(jnp.float32)
+            value = addend if value is None else value + addend
+        out[i] = value.astype(out.dtype)
+
+
+def gathered(parts, side):
+    return pl.pallas_call(
+        functools.partial(gathered_kernel, side),
+        out_shape=pltpu.VMEM(parts[0].shape, parts[0].dtype),
+        in_specs=[VMEM] * len(parts),
+        out_specs=VMEM,
+        compiler_params=PARAMS,
+        name="gathered",
+    )(*[near(p) for p in parts])
+
+
+def total(parts):
+    out = parts[0].astype(jnp.float32)
+    for part in parts[1:]:
+        out = out + part.astype(jnp.float32)
+    return out.astype(jnp.bfloat16)
+
+
+def fast(side, depth, wide_columns, tokens, grad_hidden, gate_pre, momentum):
+    nodes = 2 * side * side
+    block = momentum.shape[0] // nodes
+    columns = grad_hidden.shape[1]
+    sides, depths = range(side), range(depth)
+    wide_part, part = (0, wide_columns), (wide_columns, columns)
+
+    def chip_pairs(first, second):
+        pairs = []
+        for n in range(nodes):
+            core, x, y = n % 2, n // 2 % side, n // 2 // side
+            dx, dy = (first, second) if core == 0 else (second, first)
+            pairs.append((n, ((y ^ dy) * side + (x ^ dx)) * 2 + core))
+        return pairs
+
+    def swap(a):
+        return lax.ppermute(a, "node", [(n, n ^ 1) for n in range(nodes)])
+
+    def plane(a, first, second):
+        return lax.ppermute(a, "node", chip_pairs(first, second))
+
+    def along(a, q):
+        return lax.ppermute(a, "local", [(i, i ^ q) for i in depths])
+
+    def flat(groups):
+        return [[at for group in groups for at in group]]
+
+    def multiply(tokens, ups, addend, other, groups, of):
+        return products(tokens, ups, addend, other, groups, of, side, depth, block)
+
+    far = [[(f, s, q) for s in sides for q in depths] for f in range(1, side)]
+    close = [[(0, s, q) for s in sides for q in depths]]
+    wide = [[(f, s, q) for f in sides for s in sides] for q in depths]
+
+    far_other, up_t = multiply(tokens, (grad_hidden, gate_pre), None, True, flat(far), part)
+    far_got = swap(far_other)
+    wide_other = multiply(tokens, (up_t,), None, True, flat(wide), wide_part)[0]
+    wide_got = swap(wide_other)
+    far_sum = multiply(tokens, (up_t,), far_got, False, far, part)
+    held = [plane(a, f, 0) for f, a in enumerate(far_sum, 1)]
+    wide_sum = multiply(tokens, (up_t,), wide_got, False, wide, wide_part)
+    wide_held = [wide_sum[0]] + [along(wide_sum[q], q) for q in range(1, depth)]
+    close_up = after(up_t, wide_other, *far_sum)
+    close_other = multiply(tokens, (close_up,), None, True, close, part)[0]
+    close_got = swap(close_other)
+    held = [*multiply(tokens, (close_up,), close_got, False, close, part), *held]
+
+    sent = [plane(total([a[s * depth : (s + 1) * depth] for a in held]), 0, s) for s in range(1, side)]
+    held = [a[:depth] for a in held] + sent
+    pieces = [total([a[q] for a in held]) for q in depths]
+    wide_held = after(wide_held, *pieces[1:])
+    shard = total([pieces[0]] + [along(pieces[q], q) for q in range(1, depth)])
+
+    places = [(f, s) for f in sides for s in sides]
+    wide_shard = total(wide_held)
+    wide_all = [wide_shard if at == (0, 0) else plane(wide_shard, *at) for at in places]
+    own = [shard if at == (0, 0) else plane(shard, *at) for at in places]
+    decayed = 0.9 * momentum
+    wide_own = gathered(wide_all, side)
+    out = update(None, decayed, wide_own, own, False, side)
+    return update(out, decayed, swap(wide_own), [swap(a) for a in own], True, side)
+
+
+def plain(tokens, grad_hidden, gate_pre, momentum):
     up_grad = (grad_hidden.astype(jnp.float32) * jax.nn.silu(gate_pre.astype(jnp.float32))).astype(
         jnp.bfloat16
     )
@@ -36,13 +276,24 @@
 
 
 def solution(mesh):
+    nodes, depth = mesh.shape["node"], mesh.shape["local"]
+    side = math.isqrt(nodes // 2)
+    square = nodes == 2 * side * side and side & (side - 1) == 0 and depth & (depth - 1) == 0
+
+    def per_device(tokens, grad_hidden, gate_pre, momentum):
+        lanes = 128
+        aligned = momentum.shape[0] % (nodes * lanes) == 0 and grad_hidden.shape[1] % lanes == 0
+        if square and aligned:
+            wide = grad_hidden.shape[1] * 3 // 8 // 16 * 16
+            return fast(side, depth, wide, tokens, grad_hidden, gate_pre, momentum)
+        return plain(tokens, grad_hidden, gate_pre, momentum)
+
     in_specs = (
         P(("node", "local"), None),
         P(("node", "local"), None),
         P(("node", "local"), None),
         P("local", None),
     )
-    out_specs = P("local", None)
     return jax.shard_map(
-        per_device, mesh=mesh, in_specs=in_specs, out_specs=out_specs, check_vma=False
-    )
+        per_device, mesh=mesh, in_specs=in_specs, out_specs=P("local", None), check_vma=False
+    )

time: 148 us -> 64.9 us (0.44)
  the two profiles are of different devices: /device:TPU:0 before, /device:TPU:13 now
where the time goes in v1:
time: 64.9 us; the launch traced here: 64.7 us
  waiting for transfers between devices  32.3 us (50%)
  starting transfers between devices  23.7 us (37%)
  Pallas kernels  8.07 us (12%)
    ppermute x8, waiting for transfers between devices, plane(): return lax.ppermute(a, 'node', chip_pairs(first, second))  15.7 us
    ppermute x6, waiting for transfers between devices, along(): return lax.ppermute(a, 'local', [(i, i ^ q) for i in depths])  15.7 us
    ppermute x8, starting transfers between devices, swap(): return lax.ppermute(a, 'node', [(n, n ^ 1) for n in range(nodes)])  11.4 us
    ppermute x6, starting transfers between devices, along(): return lax.ppermute(a, 'local', [(i, i ^ q) for i in depths])  7.51 us
    pallas_call x6, Pallas kernels, products(): pl.pallas_call(functools.partial(product_kernel, side, depth, other, grou...  5.8 us
    ppermute x8, starting transfers between devices, plane(): return lax.ppermute(a, 'node', chip_pairs(first, second))  4.73 us
    pallas_call x2, Pallas kernels, update(): pl.pallas_call(functools.partial(update_kernel, side, swapped), out_shape...  2.17 us
  transfers between devices with their start and end apart: 22, of which 10 were waited for; matrix products, arithmetic and copies ran while one was open for 1% of the time, Pallas kernels for 6%

profile of v1, /device:TPU:13, one launch (start us, length us, event | category | flops | bytes accessed | tf_op | source)
XLA Modules:
  0.0 64.7 jit_solution(10663275178756481990)
XLA Ops:
  0.0 2.1 %products.6 = (bf16[8,160,256]{2,1,0:T(8,128)(2,1)S(1)}, bf16[256,256]{1,0:T(8,128)(2,1)S(1)}) custom-call(bf16[256,8192]{1,0:T(8,128)(2,1)} %refs_0_.11, bf16[256,256]{1,0:T(8,128)(2,1)} %refs_1_.1, bf16[256,256]{1,0:T(8,128)(2,1)} %refs_2_.1), custom_call_target="tpu_custom_call" | custom-call | tf_op jit(solution)/shard_map/products/pallas_call | solution.py:102
  2.1 0.7 %collective-permute-start.4 = (bf16[8,160,256]{2,1,0:T(8,128)(2,1)S(1)}, bf16[8,160,256]{2,1,0:T(8,128)(2,1)S(1)}, u32[]{:S(2)}, u32[]{:S(2)}) collective-permute-start(bf16[8,160,256]{2,1,0:T(8,128)(2,1)S(1)} %get-tuple-element.21), channel_id=1, source_target_pairs={{0,4},{4,0},{8,12},{12,8},{16,20},{20,16},{24,28},{28,24},{1,5},{5... | collective-permute-start | bytes 1966088 | tf_op jit(solution)/shard_map/ppermute | solution.py:200
  2.8 1.0 %products.7 = bf16[16,96,256]{2,1,0:T(8,128)(2,1)S(1)} custom-call(bf16[256,8192]{1,0:T(8,128)(2,1)S(1)} %copy-done, bf16[256,256]{1,0:T(8,128)(2,1)S(1)} %get-tuple-element.22.refs_1_), custom_call_target="tpu_custom_call" | custom-call | tf_op jit(solution)/shard_map/products/pallas_call | solution.py:102
  3.8 0.8 %collective-permute-done.4.refs_2_ = bf16[8,160,256]{2,1,0:T(8,128)(2,1)S(1)} collective-permute-done((bf16[8,160,256]{2,1,0:T(8,128)(2,1)S(1)}, bf16[8,160,256]{2,1,0:T(8,128)(2,1)S(1)}, u32[]{:S(2)}, u32[]{:S(2)}) %collective-permute-start.4) | collective-permute-done | bytes 655392 | tf_op jit(solution)/shard_map/ppermute | solution.py:200
  4.5 0.6 products.9
  5.1 0.6 products.10
  5.8 0.4 collective-permute-start.5
  6.2 0.2 collective-permute-start.6
  6.4 1.4 %collective-permute-start = (bf16[16,96,256]{2,1,0:T(8,128)(2,1)S(1)}, bf16[16,96,256]{2,1,0:T(8,128)(2,1)S(1)}, u32[]{:S(2)}, u32[]{:S(2)}) collective-permute-start(bf16[16,96,256]{2,1,0:T(8,128)(2,1)S(1)} %products.7), channel_id=1, source_target_pairs={{0,4},{4,0},{8,12},{12,8},{16,20},{20,16},{24,28},{28,24},{1,5},{5... | collective-permute-start | bytes 2359304 | tf_op jit(solution)/shard_map/ppermute | solution.py:200
  7.8 0.1 collective-permute-done.5.refs_2_
  7.9 0.6 products.11
  8.5 7.4 %collective-permute-done.6 = bf16[8,160,256]{2,1,0:T(8,128)(2,1)S(1)} collective-permute-done((bf16[8,160,256]{2,1,0:T(8,128)(2,1)S(1)}, bf16[8,160,256]{2,1,0:T(8,128)(2,1)S(1)}, u32[]{:S(2)}, u32[]{:S(2)}) %collective-permute-start.6) | collective-permute-done | bytes 655392 | tf_op jit(solution)/shard_map/ppermute | solution.py:203
  15.9 0.1 add_convert_fusion
  16.0 1.3 %collective-permute-start.7 = (bf16[4,160,256]{2,1,0:T(8,128)(2,1)S(1)}, bf16[4,160,256]{2,1,0:T(8,128)(2,1)S(1)}, u32[]{:S(2)}, u32[]{:S(2)}) collective-permute-start(bf16[4,160,256]{2,1,0:T(8,128)(2,1)S(1)} %add_convert_fusion), channel_id=1, source_target_pairs={{0,16},{4,12},{8,24},{12,4},{16,0},{20,28},{24,8},{28,20},{1,17},{... | collective-permute-start | bytes 983048 | tf_op jit(solution)/shard_map/ppermute | solution.py:203
  17.3 0.0 collective-permute-done.refs_2_
  17.3 1.0 %products.8 = (bf16[4,96,256]{2,1,0:T(8,128)(2,1)S(1)}, bf16[4,96,256]{2,1,0:T(8,128)(2,1)S(1)}, bf16[4,96,256]{2,1,0:T(8,128)(2,1)S(1)}, bf16[4,96,256]{2,1,0:T(8,128)(2,1)S(1)}) custom-call(bf16[256,8192]{1,0:T(8,128)(2,1)S(1)} %copy-done, bf16[256,256]{1,0:T(8,128)(2,1)S(1)} %get-tuple-element.22.refs_1_, ...), custom_call_target="tpu_custom_call" | custom-call | tf_op jit(solution)/shard_map/products/pallas_call | solution.py:102
  18.3 0.0 copy-start.1
  18.3 0.2 collective-permute-start.1
  18.5 2.3 %collective-permute-start.2 = (bf16[4,96,256]{2,1,0:T(8,128)(2,1)S(1)}, bf16[4,96,256]{2,1,0:T(8,128)(2,1)S(1)}, u32[]{:S(2)}, u32[]{:S(2)}) collective-permute-start(bf16[4,96,256]{2,1,0:T(8,128)(2,1)S(1)} %get-tuple-element.19), channel_id=1, source_target_pairs={{0,2},{1,3},{2,0},{3,1},{4,6},{5,7},{6,4},{7,5},{8,10},{9,11},{10,... | collective-permute-start | bytes 589832 | tf_op jit(solution)/shard_map/ppermute | solution.py:206
  20.8 0.2 collective-permute-start.3
  21.0 1.3 %collective-permute-done.7 = bf16[4,160,256]{2,1,0:T(8,128)(2,1)S(1)} collective-permute-done((bf16[4,160,256]{2,1,0:T(8,128)(2,1)S(1)}, bf16[4,160,256]{2,1,0:T(8,128)(2,1)S(1)}, u32[]{:S(2)}, u32[]{:S(2)}) %collective-permute-start.7) | collective-permute-done | bytes 327712 | tf_op jit(solution)/shard_map/ppermute | solution.py:203
  22.3 0.1 fusion.5
  22.4 1.4 %collective-permute-start.14 = (bf16[160,256]{1,0:T(8,128)(2,1)S(1)}, bf16[160,256]{1,0:T(8,128)(2,1)S(1)}, u32[]{:S(2)}, u32[]{:S(2)}) collective-permute-start(bf16[160,256]{1,0:T(8,128)(2,1)S(1)} %get-tuple-element.27), channel_id=1, source_target_pairs={{0,3},{1,2},{2,1},{3,0},{4,7},{5,6},{6,5},{7,4},{8,11},{9,10},{10,... | collective-permute-start | bytes 245768 | tf_op jit(solution)/shard_map/ppermute | solution.py:206
  23.8 1.1 %collective-permute-start.13 = (bf16[160,256]{1,0:T(8,128)(2,1)S(1)}, bf16[160,256]{1,0:T(8,128)(2,1)S(1)}, u32[]{:S(2)}, u32[]{:S(2)}) collective-permute-start(bf16[160,256]{1,0:T(8,128)(2,1)S(1)} %get-tuple-element.28), channel_id=1, source_target_pairs={{0,2},{1,3},{2,0},{3,1},{4,6},{5,7},{6,4},{7,5},{8,10},{9,11},{10,... | collective-permute-start | bytes 245768 | tf_op jit(solution)/shard_map/ppermute | solution.py:206
  24.9 1.6 %collective-permute-done.1 = bf16[4,96,256]{2,1,0:T(8,128)(2,1)S(1)} collective-permute-done((bf16[4,96,256]{2,1,0:T(8,128)(2,1)S(1)}, bf16[4,96,256]{2,1,0:T(8,128)(2,1)S(1)}, u32[]{:S(2)}, u32[]{:S(2)}) %collective-permute-start.1) | collective-permute-done | bytes 196640 | tf_op jit(solution)/shard_map/ppermute | solution.py:206
  26.5 2.3 %collective-permute-start.12 = (bf16[160,256]{1,0:T(8,128)(2,1)S(1)}, bf16[160,256]{1,0:T(8,128)(2,1)S(1)}, u32[]{:S(2)}, u32[]{:S(2)}) collective-permute-start(bf16[160,256]{1,0:T(8,128)(2,1)S(1)} %get-tuple-element.29), channel_id=1, source_target_pairs={{0,1},{1,0},{2,3},{3,2},{4,5},{5,4},{6,7},{7,6},{8,9},{9,8},{10,11... | collective-permute-start | bytes 245768 | tf_op jit(solution)/shard_map/ppermute | solution.py:206
  28.8 1.0 %collective-permute-done.2 = bf16[4,96,256]{2,1,0:T(8,128)(2,1)S(1)} collective-permute-done((bf16[4,96,256]{2,1,0:T(8,128)(2,1)S(1)}, bf16[4,96,256]{2,1,0:T(8,128)(2,1)S(1)}, u32[]{:S(2)}, u32[]{:S(2)}) %collective-permute-start.2) | collective-permute-done | bytes 196640 | tf_op jit(solution)/shard_map/ppermute | solution.py:206
  29.8 11.9 %collective-permute-done.3 = bf16[4,96,256]{2,1,0:T(8,128)(2,1)S(1)} collective-permute-done((bf16[4,96,256]{2,1,0:T(8,128)(2,1)S(1)}, bf16[4,96,256]{2,1,0:T(8,128)(2,1)S(1)}, u32[]{:S(2)}, u32[]{:S(2)}) %collective-permute-start.3) | collective-permute-done | bytes 196640 | tf_op jit(solution)/shard_map/ppermute | solution.py:206
  41.7 0.1 add_convert_fusion.1.refs_0_
  41.8 0.1 collective-permute-start.10
  41.9 0.4 collective-permute-start.9
  42.4 1.1 %collective-permute-done.14 = bf16[160,256]{1,0:T(8,128)(2,1)S(1)} collective-permute-done((bf16[160,256]{1,0:T(8,128)(2,1)S(1)}, bf16[160,256]{1,0:T(8,128)(2,1)S(1)}, u32[]{:S(2)}, u32[]{:S(2)}) %collective-permute-start.14) | collective-permute-done | bytes 81952 | tf_op jit(solution)/shard_map/ppermute | solution.py:206
  43.5 1.1 %collective-permute-start.8 = (bf16[4,96,256]{2,1,0:T(8,128)(2,1)S(1)}, bf16[4,96,256]{2,1,0:T(8,128)(2,1)S(1)}, u32[]{:S(2)}, u32[]{:S(2)}) collective-permute-start(bf16[4,96,256]{2,1,0:T(8,128)(2,1)S(1)} %add_convert_fusion.1.refs_0_), channel_id=1, source_target_pairs={{0,16},{4,12},{8,24},{12,4},{16,0},{20,28},{24,8},{28,20},{1,17},{... | collective-permute-start | bytes 589832 | tf_op jit(solution)/shard_map/ppermute | solution.py:203
  44.6 0.1 fusion.2.refs_2_
  44.6 0.1 collective-permute-start.20
  44.8 1.5 %collective-permute-start.18 = (bf16[160,256]{1,0:T(8,128)(2,1)S(1)}, bf16[160,256]{1,0:T(8,128)(2,1)S(1)}, u32[]{:S(2)}, u32[]{:S(2)}) collective-permute-start(bf16[160,256]{1,0:T(8,128)(2,1)S(1)} %fusion.2.refs_2_), channel_id=1, source_target_pairs={{0,8},{4,20},{8,0},{12,28},{16,24},{20,4},{24,16},{28,12},{1,9},{5... | collective-permute-start | bytes 245768 | tf_op jit(solution)/shard_map/ppermute | solution.py:203
  46.3 6.4 %collective-permute-done.20.refs_5_ = bf16[160,256]{1,0:T(8,128)(2,1)S(1)} collective-permute-done((bf16[160,256]{1,0:T(8,128)(2,1)S(1)}, bf16[160,256]{1,0:T(8,128)(2,1)S(1)}, u32[]{:S(2)}, u32[]{:S(2)}) %collective-permute-start.20) | collective-permute-done | bytes 81952 | tf_op jit(solution)/shard_map/ppermute | solution.py:203
  52.7 0.5 collective-permute-done.18.refs_4_
  53.3 3.8 %collective-permute-start.15 = (bf16[160,256]{1,0:T(8,128)(2,1)S(1)}, bf16[160,256]{1,0:T(8,128)(2,1)S(1)}, u32[]{:S(2)}, u32[]{:S(2)}) collective-permute-start(bf16[160,256]{1,0:T(8,128)(2,1)S(1)} %fusion.2.refs_2_), channel_id=1, source_target_pairs={{0,4},{4,0},{8,12},{12,8},{16,20},{20,16},{24,28},{28,24},{1,5},{5... | collective-permute-start | bytes 245768 | tf_op jit(solution)/shard_map/ppermute | solution.py:200
  57.1 4.4 %collective-permute-start.21 = (bf16[160,256]{1,0:T(8,128)(2,1)S(1)}, bf16[160,256]{1,0:T(8,128)(2,1)S(1)}, u32[]{:S(2)}, u32[]{:S(2)}) collective-permute-start(bf16[160,256]{1,0:T(8,128)(2,1)S(1)} %collective-permute-done.20.refs_5_), channel_id=1, source_target_pairs={{0,4},{4,0},{8,12},{12,8},{16,20},{20,16},{24,28},{28,24},{1,5},{5... | collective-permute-start | bytes 245768 | tf_op jit(solution)/shard_map/ppermute | solution.py:200
  61.5 0.0 collective-permute-start.19
  61.5 0.5 collective-permute-start.17
  62.0 0.1 gathered.1.refs_1_
  62.1 0.1 collective-permute-start.11
  62.3 0.2 broadcast_multiply_fusion.refs_0_
  62.4 1.1 %update.2.refs_6_ = f32[2048,256]{1,0:T(8,128)} custom-call(f32[2048,256]{1,0:T(8,128)S(1)} %broadcast_multiply_fusion.refs_0_, bf16[4,96,256]{2,1,0:T(8,128)(2,1)S(1)} %gathered.1.refs_1_, bf16[160,256]{1,0:T(8,128)(2,1)S(1)} %fusion.2.refs_2_, bf16[160,256]{1,0:T(8,128)(2,1)S(1)} %collective-permute-done.16.refs_3_, ...), custom_call_target="tpu_custom_call" | custom-call | tf_op jit(solution)/shard_map/update/pallas_call | solution.py:140
  63.6 0.0 collective-permute-done.11.refs_1_
  63.6 1.1 %update.3 = f32[2048,256]{1,0:T(8,128)} custom-call(f32[2048,256]{1,0:T(8,128)S(1)} %broadcast_multiply_fusion.refs_0_, bf16[4,96,256]{2,1,0:T(8,128)(2,1)S(1)} %collective-permute-done.11.refs_1_, bf16[160,256]{1,0:T(8,128)(2,1)S(1)} %collective-permute-done.15.refs_2_, ...), custom_call_target="tpu_custom_call", output_to_operand_aliasing={{}: (6, {})} | custom-call | tf_op jit(solution)/shard_map/update/pallas_call | solution.py:140
  (14 shorter events, 0.0 us)
Async XLA Ops:
  0.0 2.8 %copy-start = (bf16[256,8192]{1,0:T(8,128)(2,1)S(1)}, bf16[256,8192]{1,0:T(8,128)(2,1)}, u32[]{:S(2)}) copy-start(bf16[256,8192]{1,0:T(8,128)(2,1)} %refs_0_.11) | copy-start | bytes 12582916
  2.1 2.5 %collective-permute-start.4 = (bf16[8,160,256]{2,1,0:T(8,128)(2,1)S(1)}, bf16[8,160,256]{2,1,0:T(8,128)(2,1)S(1)}, u32[]{:S(2)}, u32[]{:S(2)}) collective-permute-start(bf16[8,160,256]{2,1,0:T(8,128)(2,1)S(1)} %get-tuple-element.21), channel_id=1, source_target_pairs={{0,4},{4,0},{8,12},{12,8},{16,20},{20,16},{24,28},{28,24},{1,5},{5... | collective-permute-start | bytes 1966088 | tf_op jit(solution)/shard_map/ppermute | solution.py:200
  5.8 2.2 %collective-permute-start.5 = (bf16[8,160,256]{2,1,0:T(8,128)(2,1)S(1)}, bf16[8,160,256]{2,1,0:T(8,128)(2,1)S(1)}, u32[]{:S(2)}, u32[]{:S(2)}) collective-permute-start(bf16[8,160,256]{2,1,0:T(8,128)(2,1)S(1)} %products.10), channel_id=1, source_target_pairs={{0,4},{4,0},{8,12},{12,8},{16,20},{20,16},{24,28},{28,24},{1,5},{5... | collective-permute-start | bytes 1966088 | tf_op jit(solution)/shard_map/ppermute | solution.py:200
  6.2 9.7 %collective-permute-start.6 = (bf16[8,160,256]{2,1,0:T(8,128)(2,1)S(1)}, bf16[8,160,256]{2,1,0:T(8,128)(2,1)S(1)}, u32[]{:S(2)}, u32[]{:S(2)}) collective-permute-start(bf16[8,160,256]{2,1,0:T(8,128)(2,1)S(1)} %products.9), channel_id=1, source_target_pairs={{0,8},{4,20},{8,0},{12,28},{16,24},{20,4},{24,16},{28,12},{1,9},{5... | collective-permute-start | bytes 1966088 | tf_op jit(solution)/shard_map/ppermute | solution.py:203
  6.4 10.9 %collective-permute-start = (bf16[16,96,256]{2,1,0:T(8,128)(2,1)S(1)}, bf16[16,96,256]{2,1,0:T(8,128)(2,1)S(1)}, u32[]{:S(2)}, u32[]{:S(2)}) collective-permute-start(bf16[16,96,256]{2,1,0:T(8,128)(2,1)S(1)} %products.7), channel_id=1, source_target_pairs={{0,4},{4,0},{8,12},{12,8},{16,20},{20,16},{24,28},{28,24},{1,5},{5... | collective-permute-start | bytes 2359304 | tf_op jit(solution)/shard_map/ppermute | solution.py:200
  16.0 6.3 %collective-permute-start.7 = (bf16[4,160,256]{2,1,0:T(8,128)(2,1)S(1)}, bf16[4,160,256]{2,1,0:T(8,128)(2,1)S(1)}, u32[]{:S(2)}, u32[]{:S(2)}) collective-permute-start(bf16[4,160,256]{2,1,0:T(8,128)(2,1)S(1)} %add_convert_fusion), channel_id=1, source_target_pairs={{0,16},{4,12},{8,24},{12,4},{16,0},{20,28},{24,8},{28,20},{1,17},{... | collective-permute-start | bytes 983048 | tf_op jit(solution)/shard_map/ppermute | solution.py:203
  18.3 44.0 %copy-start.1 = (f32[2048,256]{1,0:T(8,128)S(1)}, f32[2048,256]{1,0:T(8,128)}, u32[]{:S(2)}) copy-start(f32[2048,256]{1,0:T(8,128)} %param.7) | copy-start | bytes 6291460
  18.3 8.2 %collective-permute-start.1 = (bf16[4,96,256]{2,1,0:T(8,128)(2,1)S(1)}, bf16[4,96,256]{2,1,0:T(8,128)(2,1)S(1)}, u32[]{:S(2)}, u32[]{:S(2)}) collective-permute-start(bf16[4,96,256]{2,1,0:T(8,128)(2,1)S(1)} %get-tuple-element.18), channel_id=1, source_target_pairs={{0,1},{1,0},{2,3},{3,2},{4,5},{5,4},{6,7},{7,6},{8,9},{9,8},{10,11... | collective-permute-start | bytes 589832 | tf_op jit(solution)/shard_map/ppermute | solution.py:206
  18.5 11.3 %collective-permute-start.2 = (bf16[4,96,256]{2,1,0:T(8,128)(2,1)S(1)}, bf16[4,96,256]{2,1,0:T(8,128)(2,1)S(1)}, u32[]{:S(2)}, u32[]{:S(2)}) collective-permute-start(bf16[4,96,256]{2,1,0:T(8,128)(2,1)S(1)} %get-tuple-element.19), channel_id=1, source_target_pairs={{0,2},{1,3},{2,0},{3,1},{4,6},{5,7},{6,4},{7,5},{8,10},{9,11},{10,... | collective-permute-start | bytes 589832 | tf_op jit(solution)/shard_map/ppermute | solution.py:206
  20.8 20.9 %collective-permute-start.3 = (bf16[4,96,256]{2,1,0:T(8,128)(2,1)S(1)}, bf16[4,96,256]{2,1,0:T(8,128)(2,1)S(1)}, u32[]{:S(2)}, u32[]{:S(2)}) collective-permute-start(bf16[4,96,256]{2,1,0:T(8,128)(2,1)S(1)} %get-tuple-element.20), channel_id=1, source_target_pairs={{0,3},{1,2},{2,1},{3,0},{4,7},{5,6},{6,5},{7,4},{8,11},{9,10},{10,... | collective-permute-start | bytes 589832 | tf_op jit(solution)/shard_map/ppermute | solution.py:206
  22.4 21.1 %collective-permute-start.14 = (bf16[160,256]{1,0:T(8,128)(2,1)S(1)}, bf16[160,256]{1,0:T(8,128)(2,1)S(1)}, u32[]{:S(2)}, u32[]{:S(2)}) collective-permute-start(bf16[160,256]{1,0:T(8,128)(2,1)S(1)} %get-tuple-element.27), channel_id=1, source_target_pairs={{0,3},{1,2},{2,1},{3,0},{4,7},{5,6},{6,5},{7,4},{8,11},{9,10},{10,... | collective-permute-start | bytes 245768 | tf_op jit(solution)/shard_map/ppermute | solution.py:206
  23.8 20.8 %collective-permute-start.13 = (bf16[160,256]{1,0:T(8,128)(2,1)S(1)}, bf16[160,256]{1,0:T(8,128)(2,1)S(1)}, u32[]{:S(2)}, u32[]{:S(2)}) collective-permute-start(bf16[160,256]{1,0:T(8,128)(2,1)S(1)} %get-tuple-element.28), channel_id=1, source_target_pairs={{0,2},{1,3},{2,0},{3,1},{4,6},{5,7},{6,4},{7,5},{8,10},{9,11},{10,... | collective-permute-start | bytes 245768 | tf_op jit(solution)/shard_map/ppermute | solution.py:206
  26.5 18.1 %collective-permute-start.12 = (bf16[160,256]{1,0:T(8,128)(2,1)S(1)}, bf16[160,256]{1,0:T(8,128)(2,1)S(1)}, u32[]{:S(2)}, u32[]{:S(2)}) collective-permute-start(bf16[160,256]{1,0:T(8,128)(2,1)S(1)} %get-tuple-element.29), channel_id=1, source_target_pairs={{0,1},{1,0},{2,3},{3,2},{4,5},{5,4},{6,7},{7,6},{8,9},{9,8},{10,11... | collective-permute-start | bytes 245768 | tf_op jit(solution)/shard_map/ppermute | solution.py:206
  41.8 19.7 %collective-permute-start.10 = (bf16[4,96,256]{2,1,0:T(8,128)(2,1)S(1)}, bf16[4,96,256]{2,1,0:T(8,128)(2,1)S(1)}, u32[]{:S(2)}, u32[]{:S(2)}) collective-permute-start(bf16[4,96,256]{2,1,0:T(8,128)(2,1)S(1)} %add_convert_fusion.1.refs_0_), channel_id=1, source_target_pairs={{0,24},{4,28},{8,16},{12,20},{16,8},{20,12},{24,0},{28,4},{1,25},{... | collective-permute-start | bytes 589832 | tf_op jit(solution)/shard_map/ppermute | solution.py:203
  41.9 19.6 %collective-permute-start.9 = (bf16[4,96,256]{2,1,0:T(8,128)(2,1)S(1)}, bf16[4,96,256]{2,1,0:T(8,128)(2,1)S(1)}, u32[]{:S(2)}, u32[]{:S(2)}) collective-permute-start(bf16[4,96,256]{2,1,0:T(8,128)(2,1)S(1)} %add_convert_fusion.1.refs_0_), channel_id=1, source_target_pairs={{0,8},{4,20},{8,0},{12,28},{16,24},{20,4},{24,16},{28,12},{1,9},{5... | collective-permute-start | bytes 589832 | tf_op jit(solution)/shard_map/ppermute | solution.py:203
  43.5 18.5 %collective-permute-start.8 = (bf16[4,96,256]{2,1,0:T(8,128)(2,1)S(1)}, bf16[4,96,256]{2,1,0:T(8,128)(2,1)S(1)}, u32[]{:S(2)}, u32[]{:S(2)}) collective-permute-start(bf16[4,96,256]{2,1,0:T(8,128)(2,1)S(1)} %add_convert_fusion.1.refs_0_), channel_id=1, source_target_pairs={{0,16},{4,12},{8,24},{12,4},{16,0},{20,28},{24,8},{28,20},{1,17},{... | collective-permute-start | bytes 589832 | tf_op jit(solution)/shard_map/ppermute | solution.py:203
  44.6 8.1 %collective-permute-start.20 = (bf16[160,256]{1,0:T(8,128)(2,1)S(1)}, bf16[160,256]{1,0:T(8,128)(2,1)S(1)}, u32[]{:S(2)}, u32[]{:S(2)}) collective-permute-start(bf16[160,256]{1,0:T(8,128)(2,1)S(1)} %fusion.2.refs_2_), channel_id=1, source_target_pairs={{0,24},{4,28},{8,16},{12,20},{16,8},{20,12},{24,0},{28,4},{1,25},{... | collective-permute-start | bytes 245768 | tf_op jit(solution)/shard_map/ppermute | solution.py:203
  44.8 8.5 %collective-permute-start.18 = (bf16[160,256]{1,0:T(8,128)(2,1)S(1)}, bf16[160,256]{1,0:T(8,128)(2,1)S(1)}, u32[]{:S(2)}, u32[]{:S(2)}) collective-permute-start(bf16[160,256]{1,0:T(8,128)(2,1)S(1)} %fusion.2.refs_2_), channel_id=1, source_target_pairs={{0,8},{4,20},{8,0},{12,28},{16,24},{20,4},{24,16},{28,12},{1,9},{5... | collective-permute-start | bytes 245768 | tf_op jit(solution)/shard_map/ppermute | solution.py:203
  52.7 4.3 %collective-permute-start.16 = (bf16[160,256]{1,0:T(8,128)(2,1)S(1)}, bf16[160,256]{1,0:T(8,128)(2,1)S(1)}, u32[]{:S(2)}, u32[]{:S(2)}) collective-permute-start(bf16[160,256]{1,0:T(8,128)(2,1)S(1)} %fusion.2.refs_2_), channel_id=1, source_target_pairs={{0,16},{4,12},{8,24},{12,4},{16,0},{20,28},{24,8},{28,20},{1,17},{... | collective-permute-start | bytes 245768 | tf_op jit(solution)/shard_map/ppermute | solution.py:203
  53.3 10.3 %collective-permute-start.15 = (bf16[160,256]{1,0:T(8,128)(2,1)S(1)}, bf16[160,256]{1,0:T(8,128)(2,1)S(1)}, u32[]{:S(2)}, u32[]{:S(2)}) collective-permute-start(bf16[160,256]{1,0:T(8,128)(2,1)S(1)} %fusion.2.refs_2_), channel_id=1, source_target_pairs={{0,4},{4,0},{8,12},{12,8},{16,20},{20,16},{24,28},{28,24},{1,5},{5... | collective-permute-start | bytes 245768 | tf_op jit(solution)/shard_map/ppermute | solution.py:200
  57.1 6.5 %collective-permute-start.21 = (bf16[160,256]{1,0:T(8,128)(2,1)S(1)}, bf16[160,256]{1,0:T(8,128)(2,1)S(1)}, u32[]{:S(2)}, u32[]{:S(2)}) collective-permute-start(bf16[160,256]{1,0:T(8,128)(2,1)S(1)} %collective-permute-done.20.refs_5_), channel_id=1, source_target_pairs={{0,4},{4,0},{8,12},{12,8},{16,20},{20,16},{24,28},{28,24},{1,5},{5... | collective-permute-start | bytes 245768 | tf_op jit(solution)/shard_map/ppermute | solution.py:200
  61.5 2.1 %collective-permute-start.19 = (bf16[160,256]{1,0:T(8,128)(2,1)S(1)}, bf16[160,256]{1,0:T(8,128)(2,1)S(1)}, u32[]{:S(2)}, u32[]{:S(2)}) collective-permute-start(bf16[160,256]{1,0:T(8,128)(2,1)S(1)} %collective-permute-done.18.refs_4_), channel_id=1, source_target_pairs={{0,4},{4,0},{8,12},{12,8},{16,20},{20,16},{24,28},{28,24},{1,5},{5... | collective-permute-start | bytes 245768 | tf_op jit(solution)/shard_map/ppermute | solution.py:200
  61.5 2.1 %collective-permute-start.17 = (bf16[160,256]{1,0:T(8,128)(2,1)S(1)}, bf16[160,256]{1,0:T(8,128)(2,1)S(1)}, u32[]{:S(2)}, u32[]{:S(2)}) collective-permute-start(bf16[160,256]{1,0:T(8,128)(2,1)S(1)} %collective-permute-done.16.refs_3_), channel_id=1, source_target_pairs={{0,4},{4,0},{8,12},{12,8},{16,20},{20,16},{24,28},{28,24},{1,5},{5... | collective-permute-start | bytes 245768 | tf_op jit(solution)/shard_map/ppermute | solution.py:200
  62.1 1.5 %collective-permute-start.11 = (bf16[4,96,256]{2,1,0:T(8,128)(2,1)S(1)}, bf16[4,96,256]{2,1,0:T(8,128)(2,1)S(1)}, u32[]{:S(2)}, u32[]{:S(2)}) collective-permute-start(bf16[4,96,256]{2,1,0:T(8,128)(2,1)S(1)} %gathered.1.refs_1_), channel_id=1, source_target_pairs={{0,4},{4,0},{8,12},{12,8},{16,20},{20,16},{24,28},{28,24},{1,5},{5... | collective-permute-start | bytes 589832 | tf_op jit(solution)/shard_map/ppermute | solution.py:200

commit v2 on v1

--- a/solution.py
+++ b/solution.py
@@ -116,7 +116,7 @@
 
 def update_kernel(side, swapped, *refs):
     chips = side * side
-    momentum, wide, *pieces = refs[: 2 + chips]
+    momentum, *pieces = refs[: 1 + chips]
     out, held, sems = refs[-3:]
     core, x, y, _ = position(side)
     block = momentum.shape[0] // (2 * chips)
@@ -125,53 +125,53 @@
     for i in range(chips):
         start = (c * chips + place(c, x, y, i // side, i % side, side)) * block
         rows = pl.ds(pl.multiple_of(start, block), block)
-        reduced = jnp.concatenate([wide[i], pieces[i][...]], axis=0)
-        held[i] = momentum[rows, :] + reduced.T.astype(jnp.float32)
+        held[i] = 0.9 * momentum[rows, :] + pieces[i][...].astype(jnp.float32)
         copies.append(pltpu.make_async_copy(held.at[i], out.at[rows, :], sems.at[i]))
         copies[-1].start()
     for copy in copies:
         copy.wait()
 
 
-def update(out, momentum, wide, pieces, swapped, side):
+def update(out, momentum, pieces, swapped, side):
     again = [] if out is None else [out]
     rows, columns = momentum.shape
     chips = len(pieces)
     return pl.pallas_call(
         functools.partial(update_kernel, side, swapped),
         out_shape=jax.ShapeDtypeStruct(momentum.shape, momentum.dtype),
-        in_specs=[VMEM] * (2 + chips) + [HBM] * len(again),
+        in_specs=[VMEM] * (1 + chips) + [HBM] * len(again),
         out_specs=HBM,
-        input_output_aliases={2 + chips: 0} if again else {},
+        input_output_aliases={1 + chips: 0} if again else {},
         scratch_shapes=[
             pltpu.VMEM((chips, rows // (2 * chips), columns), jnp.float32),
             pltpu.SemaphoreType.DMA((chips,)),
         ],
         compiler_params=PARAMS,
         name="update",
-    )(near(momentum), near(wide), *[near(p) for p in pieces], *again)
-
-
-def gathered_kernel(side, *refs):
+    )(near(momentum), *[near(p) for p in pieces], *again)
+
+
+def turned_kernel(wide_parts, *refs):
     *parts, out = refs
-    for i in range(len(parts)):
-        value = None
-        for k, part in enumerate(parts):
-            f, s = i // side ^ k // side, i % side ^ k % side
-            addend = part[f * side + s].astype(jnp.float32)
-            value = addend if value is None else value + addend
-        out[i] = value.astype(out.dtype)
-
-
-def gathered(parts, side):
+    sums = []
+    for group in (parts[:wide_parts], parts[wide_parts:]):
+        value = group[0][...].astype(jnp.float32)
+        for part in group[1:]:
+            value += part[...].astype(jnp.float32)
+        sums.append(value.astype(out.dtype))
+    out[...] = jnp.concatenate(sums, axis=0).T
+
+
+def turned(wide_parts, parts):
+    columns = wide_parts[0].shape[0] + parts[0].shape[0]
     return pl.pallas_call(
-        functools.partial(gathered_kernel, side),
-        out_shape=pltpu.VMEM(parts[0].shape, parts[0].dtype),
-        in_specs=[VMEM] * len(parts),
+        functools.partial(turned_kernel, len(wide_parts)),
+        out_shape=pltpu.VMEM((parts[0].shape[1], columns), parts[0].dtype),
+        in_specs=[VMEM] * (len(wide_parts) + len(parts)),
         out_specs=VMEM,
         compiler_params=PARAMS,
-        name="gathered",
-    )(*[near(p) for p in parts])
+        name="turned",
+    )(*[near(p) for p in (*wide_parts, *parts)])
 
 
 def total(parts):
@@ -232,16 +232,15 @@
     held = [a[:depth] for a in held] + sent
     pieces = [total([a[q] for a in held]) for q in depths]
     wide_held = after(wide_held, *pieces[1:])
-    shard = total([pieces[0]] + [along(pieces[q], q) for q in range(1, depth)])
+    pieces = pieces[:1] + [along(pieces[q], q) for q in range(1, depth)]
 
     places = [(f, s) for f in sides for s in sides]
-    wide_shard = total(wide_held)
-    wide_all = [wide_shard if at == (0, 0) else plane(wide_shard, *at) for at in places]
+    blocks = [total([a[i] for a in wide_held]) for i in range(len(places))]
+    blocks = blocks[:1] + [plane(a, *at) for a, at in zip(blocks[1:], places[1:])]
+    shard = turned(blocks, pieces)
     own = [shard if at == (0, 0) else plane(shard, *at) for at in places]
-    decayed = 0.9 * momentum
-    wide_own = gathered(wide_all, side)
-    out = update(None, decayed, wide_own, own, False, side)
-    return update(out, decayed, swap(wide_own), [swap(a) for a in own], True, side)
+    out = update(None, momentum, own, False, side)
+    return update(out, momentum, [swap(a) for a in own], True, side)
 
 
 def plain(tokens, grad_hidden, gate_pre, momentum):
@@ -284,7 +283,7 @@
         lanes = 128
         aligned = momentum.shape[0] % (nodes * lanes) == 0 and grad_hidden.shape[1] % lanes == 0
         if square and aligned:
-            wide = grad_hidden.shape[1] * 3 // 8 // 16 * 16
+            wide = grad_hidden.shape[1] * 5 // 16 // 16 * 16
             return fast(side, depth, wide, tokens, grad_hidden, gate_pre, momentum)
         return plain(tokens, grad_hidden, gate_pre, momentum)
 

time: 64.9 us -> 63.9 us (0.985)
  the two profiles are of different devices: /device:TPU:13 before, /device:TPU:17 now
where the time goes in v2:
time: 63.9 us; the launch traced here: 63.7 us
  starting transfers between devices  28 us (44%)
  waiting for transfers between devices  27 us (42%)
  Pallas kernels  8.22 us (13%)
    ppermute x8, waiting for transfers between devices, plane(): return lax.ppermute(a, 'node', chip_pairs(first, second))  14 us
    ppermute x7, starting transfers between devices, swap(): return lax.ppermute(a, 'node', [(n, n ^ 1) for n in range(nodes)])  13.2 us
    ppermute x6, waiting for transfers between devices, along(): return lax.ppermute(a, 'local', [(i, i ^ q) for i in depths])  12 us
    ppermute x8, starting transfers between devices, plane(): return lax.ppermute(a, 'node', chip_pairs(first, second))  8.08 us
    ppermute x6, starting transfers between devices, along(): return lax.ppermute(a, 'local', [(i, i ^ q) for i in depths])  6.8 us
    pallas_call x6, Pallas kernels, products(): pl.pallas_call(functools.partial(product_kernel, side, depth, other, grou...  6.02 us
    pallas_call x2, Pallas kernels, update(): pl.pallas_call(functools.partial(update_kernel, side, swapped), out_shape...  2.08 us
  transfers between devices with their start and end apart: 21, of which 7 were waited for; matrix products, arithmetic and copies ran while one was open for 0% of the time, Pallas kernels for 6%

profile of v2, /device:TPU:17, one launch (start us, length us, event | category | flops | bytes accessed | tf_op | source)
XLA Modules:
  0.0 63.7 jit_solution(11365273838250122673)
XLA Ops:
  0.0 2.1 %products.6 = (bf16[8,176,256]{2,1,0:T(8,128)(2,1)S(1)}, bf16[256,256]{1,0:T(8,128)(2,1)S(1)}) custom-call(bf16[256,8192]{1,0:T(8,128)(2,1)} %refs_0_.13, bf16[256,256]{1,0:T(8,128)(2,1)} %refs_1_.1, bf16[256,256]{1,0:T(8,128)(2,1)} %refs_2_.1), custom_call_target="tpu_custom_call" | custom-call | tf_op jit(solution)/shard_map/products/pallas_call | solution.py:102
  2.1 0.7 %collective-permute-start.4 = (bf16[8,176,256]{2,1,0:T(8,128)(2,1)S(1)}, bf16[8,176,256]{2,1,0:T(8,128)(2,1)S(1)}, u32[]{:S(2)}, u32[]{:S(2)}) collective-permute-start(bf16[8,176,256]{2,1,0:T(8,128)(2,1)S(1)} %get-tuple-element.21), channel_id=1, source_target_pairs={{0,4},{4,0},{8,12},{12,8},{16,20},{20,16},{24,28},{28,24},{1,5},{5... | collective-permute-start | bytes 2162696 | tf_op jit(solution)/shard_map/ppermute | solution.py:200
  2.8 1.0 %products.7 = bf16[16,80,256]{2,1,0:T(8,128)(2,1)S(1)} custom-call(bf16[256,8192]{1,0:T(8,128)(2,1)S(1)} %copy-done, bf16[256,256]{1,0:T(8,128)(2,1)S(1)} %get-tuple-element.22.refs_1_), custom_call_target="tpu_custom_call" | custom-call | tf_op jit(solution)/shard_map/products/pallas_call | solution.py:102
  3.9 0.8 %collective-permute-done.4.refs_2_ = bf16[8,176,256]{2,1,0:T(8,128)(2,1)S(1)} collective-permute-done((bf16[8,176,256]{2,1,0:T(8,128)(2,1)S(1)}, bf16[8,176,256]{2,1,0:T(8,128)(2,1)S(1)}, u32[]{:S(2)}, u32[]{:S(2)}) %collective-permute-start.4) | collective-permute-done | bytes 720928 | tf_op jit(solution)/shard_map/ppermute | solution.py:200
  4.7 0.6 products.9
  5.3 0.6 %products.10 = bf16[8,176,256]{2,1,0:T(8,128)(2,1)S(1)} custom-call(bf16[256,8192]{1,0:T(8,128)(2,1)S(1)} %copy-done, bf16[256,256]{1,0:T(8,128)(2,1)S(1)} %get-tuple-element.22.refs_1_), custom_call_target="tpu_custom_call" | custom-call | tf_op jit(solution)/shard_map/products/pallas_call | solution.py:102
  5.9 0.4 collective-permute-start.5
  6.4 1.2 %collective-permute-start.6 = (bf16[8,176,256]{2,1,0:T(8,128)(2,1)S(1)}, bf16[8,176,256]{2,1,0:T(8,128)(2,1)S(1)}, u32[]{:S(2)}, u32[]{:S(2)}) collective-permute-start(bf16[8,176,256]{2,1,0:T(8,128)(2,1)S(1)} %products.9), channel_id=1, source_target_pairs={{0,8},{4,20},{8,0},{12,28},{16,24},{20,4},{24,16},{28,12},{1,9},{5... | collective-permute-start | bytes 2162696 | tf_op jit(solution)/shard_map/ppermute | solution.py:203
  7.6 0.4 collective-permute-start
  8.0 0.2 collective-permute-done.5.refs_2_
  8.2 0.6 products.11
  8.8 8.0 %collective-permute-done.6 = bf16[8,176,256]{2,1,0:T(8,128)(2,1)S(1)} collective-permute-done((bf16[8,176,256]{2,1,0:T(8,128)(2,1)S(1)}, bf16[8,176,256]{2,1,0:T(8,128)(2,1)S(1)}, u32[]{:S(2)}, u32[]{:S(2)}) %collective-permute-start.6) | collective-permute-done | bytes 720928 | tf_op jit(solution)/shard_map/ppermute | solution.py:203
  16.8 0.1 add_convert_fusion
  16.9 1.3 %collective-permute-start.7 = (bf16[4,176,256]{2,1,0:T(8,128)(2,1)S(1)}, bf16[4,176,256]{2,1,0:T(8,128)(2,1)S(1)}, u32[]{:S(2)}, u32[]{:S(2)}) collective-permute-start(bf16[4,176,256]{2,1,0:T(8,128)(2,1)S(1)} %add_convert_fusion), channel_id=1, source_target_pairs={{0,16},{4,12},{8,24},{12,4},{16,0},{20,28},{24,8},{28,20},{1,17},{... | collective-permute-start | bytes 1081352 | tf_op jit(solution)/shard_map/ppermute | solution.py:203
  18.2 1.0 %products.8 = (bf16[4,80,256]{2,1,0:T(8,128)(2,1)S(1)}, bf16[4,80,256]{2,1,0:T(8,128)(2,1)S(1)}, bf16[4,80,256]{2,1,0:T(8,128)(2,1)S(1)}, bf16[4,80,256]{2,1,0:T(8,128)(2,1)S(1)}) custom-call(bf16[256,8192]{1,0:T(8,128)(2,1)S(1)} %copy-done, bf16[256,256]{1,0:T(8,128)(2,1)S(1)} %get-tuple-element.22.refs_1_, ...), custom_call_target="tpu_custom_call" | custom-call | tf_op jit(solution)/shard_map/products/pallas_call | solution.py:102
  19.2 0.0 copy-start.1
  19.3 1.4 %collective-permute-start.1 = (bf16[4,80,256]{2,1,0:T(8,128)(2,1)S(1)}, bf16[4,80,256]{2,1,0:T(8,128)(2,1)S(1)}, u32[]{:S(2)}, u32[]{:S(2)}) collective-permute-start(bf16[4,80,256]{2,1,0:T(8,128)(2,1)S(1)} %get-tuple-element.18), channel_id=1, source_target_pairs={{0,1},{1,0},{2,3},{3,2},{4,5},{5,4},{6,7},{7,6},{8,9},{9,8},{10,11... | collective-permute-start | bytes 491528 | tf_op jit(solution)/shard_map/ppermute | solution.py:206
  20.6 0.1 collective-permute-start.2
  20.7 1.3 %collective-permute-start.3 = (bf16[4,80,256]{2,1,0:T(8,128)(2,1)S(1)}, bf16[4,80,256]{2,1,0:T(8,128)(2,1)S(1)}, u32[]{:S(2)}, u32[]{:S(2)}) collective-permute-start(bf16[4,80,256]{2,1,0:T(8,128)(2,1)S(1)} %get-tuple-element.20), channel_id=1, source_target_pairs={{0,3},{1,2},{2,1},{3,0},{4,7},{5,6},{6,5},{7,4},{8,11},{9,10},{10,... | collective-permute-start | bytes 491528 | tf_op jit(solution)/shard_map/ppermute | solution.py:206
  22.0 1.6 %collective-permute-done.7 = bf16[4,176,256]{2,1,0:T(8,128)(2,1)S(1)} collective-permute-done((bf16[4,176,256]{2,1,0:T(8,128)(2,1)S(1)}, bf16[4,176,256]{2,1,0:T(8,128)(2,1)S(1)}, u32[]{:S(2)}, u32[]{:S(2)}) %collective-permute-start.7) | collective-permute-done | bytes 360480 | tf_op jit(solution)/shard_map/ppermute | solution.py:203
  23.5 0.1 fusion.3
  23.7 0.2 collective-permute-start.13
  23.9 3.2 %collective-permute-start.12 = (bf16[176,256]{1,0:T(8,128)(2,1)S(1)}, bf16[176,256]{1,0:T(8,128)(2,1)S(1)}, u32[]{:S(2)}, u32[]{:S(2)}) collective-permute-start(bf16[176,256]{1,0:T(8,128)(2,1)S(1)} %get-tuple-element.29), channel_id=1, source_target_pairs={{0,2},{1,3},{2,0},{3,1},{4,6},{5,7},{6,4},{7,5},{8,10},{9,11},{10,... | collective-permute-start | bytes 270344 | tf_op jit(solution)/shard_map/ppermute | solution.py:206
  27.1 0.0 collective-permute-done.1
  27.1 0.6 %collective-permute-start.11 = (bf16[176,256]{1,0:T(8,128)(2,1)S(1)}, bf16[176,256]{1,0:T(8,128)(2,1)S(1)}, u32[]{:S(2)}, u32[]{:S(2)}) collective-permute-start(bf16[176,256]{1,0:T(8,128)(2,1)S(1)} %get-tuple-element.30), channel_id=1, source_target_pairs={{0,1},{1,0},{2,3},{3,2},{4,5},{5,4},{6,7},{7,6},{8,9},{9,8},{10,11... | collective-permute-start | bytes 270344 | tf_op jit(solution)/shard_map/ppermute | solution.py:206
  27.8 0.0 collective-permute-done.2
  27.8 12.0 %collective-permute-done.3 = bf16[4,80,256]{2,1,0:T(8,128)(2,1)S(1)} collective-permute-done((bf16[4,80,256]{2,1,0:T(8,128)(2,1)S(1)}, bf16[4,80,256]{2,1,0:T(8,128)(2,1)S(1)}, u32[]{:S(2)}, u32[]{:S(2)}) %collective-permute-start.3) | collective-permute-done | bytes 163872 | tf_op jit(solution)/shard_map/ppermute | solution.py:206
  39.7 0.1 fusion.7
  39.8 1.2 %collective-permute-start.10 = (bf16[80,256]{1,0:T(8,128)(2,1)S(1)}, bf16[80,256]{1,0:T(8,128)(2,1)S(1)}, u32[]{:S(2)}, u32[]{:S(2)}) collective-permute-start(bf16[80,256]{1,0:T(8,128)(2,1)S(1)} %get-tuple-element.31), channel_id=1, source_target_pairs={{0,24},{4,28},{8,16},{12,20},{16,8},{20,12},{24,0},{28,4},{1,25},{... | collective-permute-start | bytes 122888 | tf_op jit(solution)/shard_map/ppermute | solution.py:203
  41.0 0.6 collective-permute-start.9
  41.6 2.0 %collective-permute-done.10.refs_3_ = bf16[80,256]{1,0:T(8,128)(2,1)S(1)} collective-permute-done((bf16[80,256]{1,0:T(8,128)(2,1)S(1)}, bf16[80,256]{1,0:T(8,128)(2,1)S(1)}, u32[]{:S(2)}, u32[]{:S(2)}) %collective-permute-start.10) | collective-permute-done | bytes 40992 | tf_op jit(solution)/shard_map/ppermute | solution.py:203
  43.7 0.5 collective-permute-start.8
  44.1 2.4 %collective-permute-done.8.refs_1_ = bf16[80,256]{1,0:T(8,128)(2,1)S(1)} collective-permute-done((bf16[80,256]{1,0:T(8,128)(2,1)S(1)}, bf16[80,256]{1,0:T(8,128)(2,1)S(1)}, u32[]{:S(2)}, u32[]{:S(2)}) %collective-permute-start.8) | collective-permute-done | bytes 40992 | tf_op jit(solution)/shard_map/ppermute | solution.py:203
  46.5 0.0 collective-permute-done.13.refs_7_
  46.5 0.0 collective-permute-done.12.refs_6_
  46.5 0.0 collective-permute-done.11.refs_5_
  46.5 0.1 turned.1.refs_1_
  46.7 2.1 %collective-permute-start.19 = (bf16[256,256]{1,0:T(8,128)(2,1)S(1)}, bf16[256,256]{1,0:T(8,128)(2,1)S(1)}, u32[]{:S(2)}, u32[]{:S(2)}) collective-permute-start(bf16[256,256]{1,0:T(8,128)(2,1)S(1)} %turned.1.refs_1_), channel_id=1, source_target_pairs={{0,24},{4,28},{8,16},{12,20},{16,8},{20,12},{24,0},{28,4},{1,25},{... | collective-permute-start | bytes 393224 | tf_op jit(solution)/shard_map/ppermute | solution.py:203
  48.8 0.1 collective-permute-start.17
  48.9 1.1 %collective-permute-start.15 = (bf16[256,256]{1,0:T(8,128)(2,1)S(1)}, bf16[256,256]{1,0:T(8,128)(2,1)S(1)}, u32[]{:S(2)}, u32[]{:S(2)}) collective-permute-start(bf16[256,256]{1,0:T(8,128)(2,1)S(1)} %turned.1.refs_1_), channel_id=1, source_target_pairs={{0,16},{4,12},{8,24},{12,4},{16,0},{20,28},{24,8},{28,20},{1,17},{... | collective-permute-start | bytes 393224 | tf_op jit(solution)/shard_map/ppermute | solution.py:203
  50.0 6.7 %collective-permute-start.14 = (bf16[256,256]{1,0:T(8,128)(2,1)S(1)}, bf16[256,256]{1,0:T(8,128)(2,1)S(1)}, u32[]{:S(2)}, u32[]{:S(2)}) collective-permute-start(bf16[256,256]{1,0:T(8,128)(2,1)S(1)} %turned.1.refs_1_), channel_id=1, source_target_pairs={{0,4},{4,0},{8,12},{12,8},{16,20},{20,16},{24,28},{28,24},{1,5},{5... | collective-permute-start | bytes 393224 | tf_op jit(solution)/shard_map/ppermute | solution.py:200
  56.7 0.0 collective-permute-done.19.refs_4_
  56.7 2.4 %collective-permute-start.20 = (bf16[256,256]{1,0:T(8,128)(2,1)S(1)}, bf16[256,256]{1,0:T(8,128)(2,1)S(1)}, u32[]{:S(2)}, u32[]{:S(2)}) collective-permute-start(bf16[256,256]{1,0:T(8,128)(2,1)S(1)} %collective-permute-done.19.refs_4_), channel_id=1, source_target_pairs={{0,4},{4,0},{8,12},{12,8},{16,20},{20,16},{24,28},{28,24},{1,5},{5... | collective-permute-start | bytes 393224 | tf_op jit(solution)/shard_map/ppermute | solution.py:200
  59.1 1.9 %collective-permute-start.18 = (bf16[256,256]{1,0:T(8,128)(2,1)S(1)}, bf16[256,256]{1,0:T(8,128)(2,1)S(1)}, u32[]{:S(2)}, u32[]{:S(2)}) collective-permute-start(bf16[256,256]{1,0:T(8,128)(2,1)S(1)} %collective-permute-done.17.refs_3_), channel_id=1, source_target_pairs={{0,4},{4,0},{8,12},{12,8},{16,20},{20,16},{24,28},{28,24},{1,5},{5... | collective-permute-start | bytes 393224 | tf_op jit(solution)/shard_map/ppermute | solution.py:200
  61.0 0.0 collective-permute-done.15.refs_2_
  61.0 0.6 collective-permute-start.16
  61.6 1.0 %update.2.refs_5_ = f32[2048,256]{1,0:T(8,128)} custom-call(f32[2048,256]{1,0:T(8,128)S(1)} %copy-done.1, bf16[256,256]{1,0:T(8,128)(2,1)S(1)} %turned.1.refs_1_, bf16[256,256]{1,0:T(8,128)(2,1)S(1)} %collective-permute-done.15.refs_2_, bf16[256,256]{1,0:T(8,128)(2,1)S(1)} %collective-permute-done.17.refs_3_, ...), custom_call_target="tpu_custom_call" | custom-call | tf_op jit(solution)/shard_map/update/pallas_call | solution.py:139
  62.7 1.0 %update.3 = f32[2048,256]{1,0:T(8,128)} custom-call(f32[2048,256]{1,0:T(8,128)S(1)} %copy-done.1, bf16[256,256]{1,0:T(8,128)(2,1)S(1)} %collective-permute-done.14.refs_1_, bf16[256,256]{1,0:T(8,128)(2,1)S(1)} %collective-permute-done.16.refs_2_, bf16[256,256]{1,0:T(8,128)(2,1)S(1)} %collective-permute-done.18.refs_3_, ...), custom_call_target="tpu_custom_call", output_to_operand_aliasing={{}: (5, {})} | custom-call | tf_op jit(solution)/shard_map/update/pallas_call | solution.py:139
  (10 shorter events, 0.0 us)
Async XLA Ops:
  0.0 2.8 %copy-start = (bf16[256,8192]{1,0:T(8,128)(2,1)S(1)}, bf16[256,8192]{1,0:T(8,128)(2,1)}, u32[]{:S(2)}) copy-start(bf16[256,8192]{1,0:T(8,128)(2,1)} %refs_0_.13) | copy-start | bytes 12582916
  2.1 2.6 %collective-permute-start.4 = (bf16[8,176,256]{2,1,0:T(8,128)(2,1)S(1)}, bf16[8,176,256]{2,1,0:T(8,128)(2,1)S(1)}, u32[]{:S(2)}, u32[]{:S(2)}) collective-permute-start(bf16[8,176,256]{2,1,0:T(8,128)(2,1)S(1)} %get-tuple-element.21), channel_id=1, source_target_pairs={{0,4},{4,0},{8,12},{12,8},{16,20},{20,16},{24,28},{28,24},{1,5},{5... | collective-permute-start | bytes 2162696 | tf_op jit(solution)/shard_map/ppermute | solution.py:200
  5.9 2.3 %collective-permute-start.5 = (bf16[8,176,256]{2,1,0:T(8,128)(2,1)S(1)}, bf16[8,176,256]{2,1,0:T(8,128)(2,1)S(1)}, u32[]{:S(2)}, u32[]{:S(2)}) collective-permute-start(bf16[8,176,256]{2,1,0:T(8,128)(2,1)S(1)} %products.10), channel_id=1, source_target_pairs={{0,4},{4,0},{8,12},{12,8},{16,20},{20,16},{24,28},{28,24},{1,5},{5... | collective-permute-start | bytes 2162696 | tf_op jit(solution)/shard_map/ppermute | solution.py:200
  6.4 10.4 %collective-permute-start.6 = (bf16[8,176,256]{2,1,0:T(8,128)(2,1)S(1)}, bf16[8,176,256]{2,1,0:T(8,128)(2,1)S(1)}, u32[]{:S(2)}, u32[]{:S(2)}) collective-permute-start(bf16[8,176,256]{2,1,0:T(8,128)(2,1)S(1)} %products.9), channel_id=1, source_target_pairs={{0,8},{4,20},{8,0},{12,28},{16,24},{20,4},{24,16},{28,12},{1,9},{5... | collective-permute-start | bytes 2162696 | tf_op jit(solution)/shard_map/ppermute | solution.py:203
  7.6 10.6 %collective-permute-start = (bf16[16,80,256]{2,1,0:T(8,128)(2,1)S(1)}, bf16[16,80,256]{2,1,0:T(8,128)(2,1)S(1)}, u32[]{:S(2)}, u32[]{:S(2)}) collective-permute-start(bf16[16,80,256]{2,1,0:T(8,128)(2,1)S(1)} %products.7), channel_id=1, source_target_pairs={{0,4},{4,0},{8,12},{12,8},{16,20},{20,16},{24,28},{28,24},{1,5},{5... | collective-permute-start | bytes 1966088 | tf_op jit(solution)/shard_map/ppermute | solution.py:200
  16.9 6.6 %collective-permute-start.7 = (bf16[4,176,256]{2,1,0:T(8,128)(2,1)S(1)}, bf16[4,176,256]{2,1,0:T(8,128)(2,1)S(1)}, u32[]{:S(2)}, u32[]{:S(2)}) collective-permute-start(bf16[4,176,256]{2,1,0:T(8,128)(2,1)S(1)} %add_convert_fusion), channel_id=1, source_target_pairs={{0,16},{4,12},{8,24},{12,4},{16,0},{20,28},{24,8},{28,20},{1,17},{... | collective-permute-start | bytes 1081352 | tf_op jit(solution)/shard_map/ppermute | solution.py:203
  19.2 42.3 %copy-start.1 = (f32[2048,256]{1,0:T(8,128)S(1)}, f32[2048,256]{1,0:T(8,128)}, u32[]{:S(2)}) copy-start(f32[2048,256]{1,0:T(8,128)} %refs_0_.15) | copy-start | bytes 6291460
  19.3 7.9 %collective-permute-start.1 = (bf16[4,80,256]{2,1,0:T(8,128)(2,1)S(1)}, bf16[4,80,256]{2,1,0:T(8,128)(2,1)S(1)}, u32[]{:S(2)}, u32[]{:S(2)}) collective-permute-start(bf16[4,80,256]{2,1,0:T(8,128)(2,1)S(1)} %get-tuple-element.18), channel_id=1, source_target_pairs={{0,1},{1,0},{2,3},{3,2},{4,5},{5,4},{6,7},{7,6},{8,9},{9,8},{10,11... | collective-permute-start | bytes 491528 | tf_op jit(solution)/shard_map/ppermute | solution.py:206
  20.6 7.2 %collective-permute-start.2 = (bf16[4,80,256]{2,1,0:T(8,128)(2,1)S(1)}, bf16[4,80,256]{2,1,0:T(8,128)(2,1)S(1)}, u32[]{:S(2)}, u32[]{:S(2)}) collective-permute-start(bf16[4,80,256]{2,1,0:T(8,128)(2,1)S(1)} %get-tuple-element.19), channel_id=1, source_target_pairs={{0,2},{1,3},{2,0},{3,1},{4,6},{5,7},{6,4},{7,5},{8,10},{9,11},{10,... | collective-permute-start | bytes 491528 | tf_op jit(solution)/shard_map/ppermute | solution.py:206
  20.7 19.1 %collective-permute-start.3 = (bf16[4,80,256]{2,1,0:T(8,128)(2,1)S(1)}, bf16[4,80,256]{2,1,0:T(8,128)(2,1)S(1)}, u32[]{:S(2)}, u32[]{:S(2)}) collective-permute-start(bf16[4,80,256]{2,1,0:T(8,128)(2,1)S(1)} %get-tuple-element.20), channel_id=1, source_target_pairs={{0,3},{1,2},{2,1},{3,0},{4,7},{5,6},{6,5},{7,4},{8,11},{9,10},{10,... | collective-permute-start | bytes 491528 | tf_op jit(solution)/shard_map/ppermute | solution.py:206
  23.7 22.8 %collective-permute-start.13 = (bf16[176,256]{1,0:T(8,128)(2,1)S(1)}, bf16[176,256]{1,0:T(8,128)(2,1)S(1)}, u32[]{:S(2)}, u32[]{:S(2)}) collective-permute-start(bf16[176,256]{1,0:T(8,128)(2,1)S(1)} %get-tuple-element.28), channel_id=1, source_target_pairs={{0,3},{1,2},{2,1},{3,0},{4,7},{5,6},{6,5},{7,4},{8,11},{9,10},{10,... | collective-permute-start | bytes 270344 | tf_op jit(solution)/shard_map/ppermute | solution.py:206
  23.9 22.6 %collective-permute-start.12 = (bf16[176,256]{1,0:T(8,128)(2,1)S(1)}, bf16[176,256]{1,0:T(8,128)(2,1)S(1)}, u32[]{:S(2)}, u32[]{:S(2)}) collective-permute-start(bf16[176,256]{1,0:T(8,128)(2,1)S(1)} %get-tuple-element.29), channel_id=1, source_target_pairs={{0,2},{1,3},{2,0},{3,1},{4,6},{5,7},{6,4},{7,5},{8,10},{9,11},{10,... | collective-permute-start | bytes 270344 | tf_op jit(solution)/shard_map/ppermute | solution.py:206
  27.1 19.4 %collective-permute-start.11 = (bf16[176,256]{1,0:T(8,128)(2,1)S(1)}, bf16[176,256]{1,0:T(8,128)(2,1)S(1)}, u32[]{:S(2)}, u32[]{:S(2)}) collective-permute-start(bf16[176,256]{1,0:T(8,128)(2,1)S(1)} %get-tuple-element.30), channel_id=1, source_target_pairs={{0,1},{1,0},{2,3},{3,2},{4,5},{5,4},{6,7},{7,6},{8,9},{9,8},{10,11... | collective-permute-start | bytes 270344 | tf_op jit(solution)/shard_map/ppermute | solution.py:206
  39.8 3.8 %collective-permute-start.10 = (bf16[80,256]{1,0:T(8,128)(2,1)S(1)}, bf16[80,256]{1,0:T(8,128)(2,1)S(1)}, u32[]{:S(2)}, u32[]{:S(2)}) collective-permute-start(bf16[80,256]{1,0:T(8,128)(2,1)S(1)} %get-tuple-element.31), channel_id=1, source_target_pairs={{0,24},{4,28},{8,16},{12,20},{16,8},{20,12},{24,0},{28,4},{1,25},{... | collective-permute-start | bytes 122888 | tf_op jit(solution)/shard_map/ppermute | solution.py:203
  41.0 3.1 %collective-permute-start.9 = (bf16[80,256]{1,0:T(8,128)(2,1)S(1)}, bf16[80,256]{1,0:T(8,128)(2,1)S(1)}, u32[]{:S(2)}, u32[]{:S(2)}) collective-permute-start(bf16[80,256]{1,0:T(8,128)(2,1)S(1)} %get-tuple-element.32), channel_id=1, source_target_pairs={{0,8},{4,20},{8,0},{12,28},{16,24},{20,4},{24,16},{28,12},{1,9},{5... | collective-permute-start | bytes 122888 | tf_op jit(solution)/shard_map/ppermute | solution.py:203
  43.7 2.9 %collective-permute-start.8 = (bf16[80,256]{1,0:T(8,128)(2,1)S(1)}, bf16[80,256]{1,0:T(8,128)(2,1)S(1)}, u32[]{:S(2)}, u32[]{:S(2)}) collective-permute-start(bf16[80,256]{1,0:T(8,128)(2,1)S(1)} %get-tuple-element.33), channel_id=1, source_target_pairs={{0,16},{4,12},{8,24},{12,4},{16,0},{20,28},{24,8},{28,20},{1,17},{... | collective-permute-start | bytes 122888 | tf_op jit(solution)/shard_map/ppermute | solution.py:203
  46.7 10.0 %collective-permute-start.19 = (bf16[256,256]{1,0:T(8,128)(2,1)S(1)}, bf16[256,256]{1,0:T(8,128)(2,1)S(1)}, u32[]{:S(2)}, u32[]{:S(2)}) collective-permute-start(bf16[256,256]{1,0:T(8,128)(2,1)S(1)} %turned.1.refs_1_), channel_id=1, source_target_pairs={{0,24},{4,28},{8,16},{12,20},{16,8},{20,12},{24,0},{28,4},{1,25},{... | collective-permute-start | bytes 393224 | tf_op jit(solution)/shard_map/ppermute | solution.py:203
  48.8 10.3 %collective-permute-start.17 = (bf16[256,256]{1,0:T(8,128)(2,1)S(1)}, bf16[256,256]{1,0:T(8,128)(2,1)S(1)}, u32[]{:S(2)}, u32[]{:S(2)}) collective-permute-start(bf16[256,256]{1,0:T(8,128)(2,1)S(1)} %turned.1.refs_1_), channel_id=1, source_target_pairs={{0,8},{4,20},{8,0},{12,28},{16,24},{20,4},{24,16},{28,12},{1,9},{5... | collective-permute-start | bytes 393224 | tf_op jit(solution)/shard_map/ppermute | solution.py:203
  48.9 12.1 %collective-permute-start.15 = (bf16[256,256]{1,0:T(8,128)(2,1)S(1)}, bf16[256,256]{1,0:T(8,128)(2,1)S(1)}, u32[]{:S(2)}, u32[]{:S(2)}) collective-permute-start(bf16[256,256]{1,0:T(8,128)(2,1)S(1)} %turned.1.refs_1_), channel_id=1, source_target_pairs={{0,16},{4,12},{8,24},{12,4},{16,0},{20,28},{24,8},{28,20},{1,17},{... | collective-permute-start | bytes 393224 | tf_op jit(solution)/shard_map/ppermute | solution.py:203
  50.0 12.7 %collective-permute-start.14 = (bf16[256,256]{1,0:T(8,128)(2,1)S(1)}, bf16[256,256]{1,0:T(8,128)(2,1)S(1)}, u32[]{:S(2)}, u32[]{:S(2)}) collective-permute-start(bf16[256,256]{1,0:T(8,128)(2,1)S(1)} %turned.1.refs_1_), channel_id=1, source_target_pairs={{0,4},{4,0},{8,12},{12,8},{16,20},{20,16},{24,28},{28,24},{1,5},{5... | collective-permute-start | bytes 393224 | tf_op jit(solution)/shard_map/ppermute | solution.py:200
  56.7 6.0 %collective-permute-start.20 = (bf16[256,256]{1,0:T(8,128)(2,1)S(1)}, bf16[256,256]{1,0:T(8,128)(2,1)S(1)}, u32[]{:S(2)}, u32[]{:S(2)}) collective-permute-start(bf16[256,256]{1,0:T(8,128)(2,1)S(1)} %collective-permute-done.19.refs_4_), channel_id=1, source_target_pairs={{0,4},{4,0},{8,12},{12,8},{16,20},{20,16},{24,28},{28,24},{1,5},{5... | collective-permute-start | bytes 393224 | tf_op jit(solution)/shard_map/ppermute | solution.py:200
  59.1 3.6 %collective-permute-start.18 = (bf16[256,256]{1,0:T(8,128)(2,1)S(1)}, bf16[256,256]{1,0:T(8,128)(2,1)S(1)}, u32[]{:S(2)}, u32[]{:S(2)}) collective-permute-start(bf16[256,256]{1,0:T(8,128)(2,1)S(1)} %collective-permute-done.17.refs_3_), channel_id=1, source_target_pairs={{0,4},{4,0},{8,12},{12,8},{16,20},{20,16},{24,28},{28,24},{1,5},{5... | collective-permute-start | bytes 393224 | tf_op jit(solution)/shard_map/ppermute | solution.py:200
  61.0 1.7 %collective-permute-start.16 = (bf16[256,256]{1,0:T(8,128)(2,1)S(1)}, bf16[256,256]{1,0:T(8,128)(2,1)S(1)}, u32[]{:S(2)}, u32[]{:S(2)}) collective-permute-start(bf16[256,256]{1,0:T(8,128)(2,1)S(1)} %collective-permute-done.15.refs_2_), channel_id=1, source_target_pairs={{0,4},{4,0},{8,12},{12,8},{16,20},{20,16},{24,28},{28,24},{1,5},{5... | collective-permute-start | bytes 393224 | tf_op jit(solution)/shard_map/ppermute | solution.py:200

commit v3 on v2

--- a/solution.py
+++ b/solution.py
@@ -155,18 +155,18 @@
     *parts, out = refs
     sums = []
     for group in (parts[:wide_parts], parts[wide_parts:]):
-        value = group[0][...].astype(jnp.float32)
+        value = group[0][0].astype(jnp.float32)
         for part in group[1:]:
-            value += part[...].astype(jnp.float32)
+            value += part[0].astype(jnp.float32)
         sums.append(value.astype(out.dtype))
     out[...] = jnp.concatenate(sums, axis=0).T
 
 
 def turned(wide_parts, parts):
-    columns = wide_parts[0].shape[0] + parts[0].shape[0]
+    columns = wide_parts[0].shape[1] + parts[0].shape[1]
     return pl.pallas_call(
         functools.partial(turned_kernel, len(wide_parts)),
-        out_shape=pltpu.VMEM((parts[0].shape[1], columns), parts[0].dtype),
+        out_shape=pltpu.VMEM((parts[0].shape[2], columns), parts[0].dtype),
         in_specs=[VMEM] * (len(wide_parts) + len(parts)),
         out_specs=VMEM,
         compiler_params=PARAMS,
@@ -211,8 +211,11 @@
     def multiply(tokens, ups, addend, other, groups, of):
         return products(tokens, ups, addend, other, groups, of, side, depth, block)
 
-    far = [[(f, s, q) for s in sides for q in depths] for f in range(1, side)]
-    close = [[(0, s, q) for s in sides for q in depths]]
+    halving = [0]
+    while len(halving) < depth:
+        halving = [2 * q for q in halving] + [2 * q + 1 for q in halving]
+    far = [[(f, s, q) for s in sides for q in halving] for f in range(1, side)]
+    close = [[(0, s, q) for s in sides for q in halving]]
     wide = [[(f, s, q) for f in sides for s in sides] for q in depths]
 
     far_other, up_t = multiply(tokens, (grad_hidden, gate_pre), None, True, flat(far), part)
@@ -229,15 +232,19 @@
     held = [*multiply(tokens, (close_up,), close_got, False, close, part), *held]
 
     sent = [plane(total([a[s * depth : (s + 1) * depth] for a in held]), 0, s) for s in range(1, side)]
-    held = [a[:depth] for a in held] + sent
-    pieces = [total([a[q] for a in held]) for q in depths]
-    wide_held = after(wide_held, *pieces[1:])
-    pieces = pieces[:1] + [along(pieces[q], q) for q in range(1, depth)]
-
+    held = held + sent
+    step, left = 1, depth
+    while left > 1:
+        left //= 2
+        sending = total([a[left : 2 * left] for a in held])
+        if left == 1:
+            wide_held = after(wide_held, sending)
+        held = held + [along(sending, step)]
+        step *= 2
     places = [(f, s) for f in sides for s in sides]
-    blocks = [total([a[i] for a in wide_held]) for i in range(len(places))]
+    blocks = [total([a[i : i + 1] for a in wide_held]) for i in range(len(places))]
     blocks = blocks[:1] + [plane(a, *at) for a, at in zip(blocks[1:], places[1:])]
-    shard = turned(blocks, pieces)
+    shard = turned(blocks, held)
     own = [shard if at == (0, 0) else plane(shard, *at) for at in places]
     out = update(None, momentum, own, False, side)
     return update(out, momentum, [swap(a) for a in own], True, side)
@@ -283,7 +290,7 @@
         lanes = 128
         aligned = momentum.shape[0] % (nodes * lanes) == 0 and grad_hidden.shape[1] % lanes == 0
         if square and aligned:
-            wide = grad_hidden.shape[1] * 5 // 16 // 16 * 16
+            wide = grad_hidden.shape[1] * 7 // 16 // 16 * 16
             return fast(side, depth, wide, tokens, grad_hidden, gate_pre, momentum)
         return plain(tokens, grad_hidden, gate_pre, momentum)
 

time: 63.9 us -> 68.8 us (1.077)
  waiting for transfers between devices: 27 us -> 33.9 us
  starting transfers between devices: 28 us -> 26.4 us
    ppermute x6 -> x5, waiting for transfers between devices: 12 us -> 19.1 us  [along(): return lax.ppermute(a, 'local', [(i, i ^ q) for i in depths])]
    ppermute x6 -> x5, starting transfers between devices: 6.8 us -> 5.11 us  [along(): return lax.ppermute(a, 'local', [(i, i ^ q) for i in depths])]
  transfers between devices with their start and end apart: 21 -> 20, of which waited for: 7 -> 9; matrix products, arithmetic and copies ran while one was open for 0% -> 0% of each run, Pallas kernels for 6% -> 5%
where the time goes in v3:
time: 68.8 us; the launch traced here: 68.7 us
  waiting for transfers between devices  33.9 us (49%)
  starting transfers between devices  26.4 us (38%)
  Pallas kernels  8.01 us (12%)
    ppermute x5, waiting for transfers between devices, along(): return lax.ppermute(a, 'local', [(i, i ^ q) for i in depths])  19.1 us
    ppermute x8, waiting for transfers between devices, plane(): return lax.ppermute(a, 'node', chip_pairs(first, second))  14.1 us
    ppermute x7, starting transfers between devices, swap(): return lax.ppermute(a, 'node', [(n, n ^ 1) for n in range(nodes)])  13.3 us
    ppermute x8, starting transfers between devices, plane(): return lax.ppermute(a, 'node', chip_pairs(first, second))  7.96 us
    pallas_call x6, Pallas kernels, products(): pl.pallas_call(functools.partial(product_kernel, side, depth, other, grou...  5.79 us
    ppermute x5, starting transfers between devices, along(): return lax.ppermute(a, 'local', [(i, i ^ q) for i in depths])  5.11 us
    pallas_call x2, Pallas kernels, update(): pl.pallas_call(functools.partial(update_kernel, side, swapped), out_shape...  2.08 us
  transfers between devices with their start and end apart: 20, of which 9 were waited for; matrix products, arithmetic and copies ran while one was open for 0% of the time, Pallas kernels for 5%

profile of v3, /device:TPU:17, one launch (start us, length us, event | category | flops | bytes accessed | tf_op | source)
XLA Modules:
  0.0 68.7 jit_solution(6478132466907703282)
XLA Ops:
  0.0 2.1 %products.6 = (bf16[8,144,256]{2,1,0:T(8,128)(2,1)S(1)}, bf16[256,256]{1,0:T(8,128)(2,1)S(1)}) custom-call(bf16[256,8192]{1,0:T(8,128)(2,1)} %refs_0_.13, bf16[256,256]{1,0:T(8,128)(2,1)} %refs_1_.1, bf16[256,256]{1,0:T(8,128)(2,1)} %refs_2_.1), custom_call_target="tpu_custom_call" | custom-call | tf_op jit(solution)/shard_map/products/pallas_call | solution.py:102
  2.1 0.7 %collective-permute-start.4 = (bf16[8,144,256]{2,1,0:T(8,128)(2,1)S(1)}, bf16[8,144,256]{2,1,0:T(8,128)(2,1)S(1)}, u32[]{:S(2)}, u32[]{:S(2)}) collective-permute-start(bf16[8,144,256]{2,1,0:T(8,128)(2,1)S(1)} %get-tuple-element.21), channel_id=1, source_target_pairs={{0,4},{4,0},{8,12},{12,8},{16,20},{20,16},{24,28},{28,24},{1,5},{5... | collective-permute-start | bytes 1769480 | tf_op jit(solution)/shard_map/ppermute | solution.py:200
  2.8 1.0 %products.7 = bf16[16,112,256]{2,1,0:T(8,128)(2,1)S(1)} custom-call(bf16[256,8192]{1,0:T(8,128)(2,1)S(1)} %copy-done, bf16[256,256]{1,0:T(8,128)(2,1)S(1)} %get-tuple-element.22.refs_1_), custom_call_target="tpu_custom_call" | custom-call | tf_op jit(solution)/shard_map/products/pallas_call | solution.py:102
  3.8 0.7 collective-permute-done.4.refs_2_
  4.4 0.6 products.9
  5.0 0.6 products.10
  5.6 0.4 collective-permute-start.5
  6.1 1.3 %collective-permute-start.6 = (bf16[8,144,256]{2,1,0:T(8,128)(2,1)S(1)}, bf16[8,144,256]{2,1,0:T(8,128)(2,1)S(1)}, u32[]{:S(2)}, u32[]{:S(2)}) collective-permute-start(bf16[8,144,256]{2,1,0:T(8,128)(2,1)S(1)} %products.9), channel_id=1, source_target_pairs={{0,8},{4,20},{8,0},{12,28},{16,24},{20,4},{24,16},{28,12},{1,9},{5... | collective-permute-start | bytes 1769480 | tf_op jit(solution)/shard_map/ppermute | solution.py:203
  7.3 0.4 collective-permute-start
  7.7 0.0 collective-permute-done.5.refs_2_
  7.7 0.6 products.11.refs_4_
  8.3 6.8 %collective-permute-done.6.refs_5_ = bf16[8,144,256]{2,1,0:T(8,128)(2,1)S(1)} collective-permute-done((bf16[8,144,256]{2,1,0:T(8,128)(2,1)S(1)}, bf16[8,144,256]{2,1,0:T(8,128)(2,1)S(1)}, u32[]{:S(2)}, u32[]{:S(2)}) %collective-permute-start.6) | collective-permute-done | bytes 589856 | tf_op jit(solution)/shard_map/ppermute | solution.py:203
  15.1 0.1 add_convert_fusion
  15.2 1.3 %collective-permute-start.7 = (bf16[4,144,256]{2,1,0:T(8,128)(2,1)S(1)}, bf16[4,144,256]{2,1,0:T(8,128)(2,1)S(1)}, u32[]{:S(2)}, u32[]{:S(2)}) collective-permute-start(bf16[4,144,256]{2,1,0:T(8,128)(2,1)S(1)} %add_convert_fusion), channel_id=1, source_target_pairs={{0,16},{4,12},{8,24},{12,4},{16,0},{20,28},{24,8},{28,20},{1,17},{... | collective-permute-start | bytes 884744 | tf_op jit(solution)/shard_map/ppermute | solution.py:203
  16.5 4.6 %collective-permute-done.7.refs_6_ = bf16[4,144,256]{2,1,0:T(8,128)(2,1)S(1)} collective-permute-done((bf16[4,144,256]{2,1,0:T(8,128)(2,1)S(1)}, bf16[4,144,256]{2,1,0:T(8,128)(2,1)S(1)}, u32[]{:S(2)}, u32[]{:S(2)}) %collective-permute-start.7) | collective-permute-done | bytes 294944 | tf_op jit(solution)/shard_map/ppermute | solution.py:203
  21.1 0.1 add_convert_fusion.1
  21.2 1.4 %collective-permute-start.8 = (bf16[2,144,256]{2,1,0:T(8,128)(2,1)S(1)}, bf16[2,144,256]{2,1,0:T(8,128)(2,1)S(1)}, u32[]{:S(2)}, u32[]{:S(2)}) collective-permute-start(bf16[2,144,256]{2,1,0:T(8,128)(2,1)S(1)} %add_convert_fusion.1), channel_id=1, source_target_pairs={{0,1},{1,0},{2,3},{3,2},{4,5},{5,4},{6,7},{7,6},{8,9},{9,8},{10,11... | collective-permute-start | bytes 442376 | tf_op jit(solution)/shard_map/ppermute | solution.py:206
  22.5 0.0 collective-permute-done.refs_2_
  22.5 1.0 %products.8 = (bf16[4,112,256]{2,1,0:T(8,128)(2,1)S(1)}, bf16[4,112,256]{2,1,0:T(8,128)(2,1)S(1)}, bf16[4,112,256]{2,1,0:T(8,128)(2,1)S(1)}, bf16[4,112,256]{2,1,0:T(8,128)(2,1)S(1)}) custom-call(bf16[256,8192]{1,0:T(8,128)(2,1)S(1)} %copy-done, bf16[256,256]{1,0:T(8,128)(2,1)S(1)} %get-tuple-element.22.refs_1_, ...), custom_call_target="tpu_custom_call" | custom-call | tf_op jit(solution)/shard_map/products/pallas_call | solution.py:102
  23.6 0.0 copy-start.1
  23.6 0.2 collective-permute-start.1
  23.8 0.0 collective-permute-start.2
  23.8 2.5 %collective-permute-start.3 = (bf16[4,112,256]{2,1,0:T(8,128)(2,1)S(1)}, bf16[4,112,256]{2,1,0:T(8,128)(2,1)S(1)}, u32[]{:S(2)}, u32[]{:S(2)}) collective-permute-start(bf16[4,112,256]{2,1,0:T(8,128)(2,1)S(1)} %get-tuple-element.20), channel_id=1, source_target_pairs={{0,3},{1,2},{2,1},{3,0},{4,7},{5,6},{6,5},{7,4},{8,11},{9,10},{10,... | collective-permute-start | bytes 688136 | tf_op jit(solution)/shard_map/ppermute | solution.py:206
  26.3 0.0 collective-permute-done.8.refs_7_
  26.3 1.0 %collective-permute-start.12 = (bf16[1,144,256]{2,1,0:T(8,128)(2,1)S(1)}, bf16[1,144,256]{2,1,0:T(8,128)(2,1)S(1)}, u32[]{:S(2)}, u32[]{:S(2)}) collective-permute-start(bf16[1,144,256]{2,1,0:T(8,128)(2,1)S(1)} %add_convert_fusion.2), channel_id=1, source_target_pairs={{0,2},{1,3},{2,0},{3,1},{4,6},{5,7},{6,4},{7,5},{8,10},{9,11},{10,... | collective-permute-start | bytes 221192 | tf_op jit(solution)/shard_map/ppermute | solution.py:206
  27.4 4.3 %collective-permute-done.1 = bf16[4,112,256]{2,1,0:T(8,128)(2,1)S(1)} collective-permute-done((bf16[4,112,256]{2,1,0:T(8,128)(2,1)S(1)}, bf16[4,112,256]{2,1,0:T(8,128)(2,1)S(1)}, u32[]{:S(2)}, u32[]{:S(2)}) %collective-permute-start.1) | collective-permute-done | bytes 229408 | tf_op jit(solution)/shard_map/ppermute | solution.py:206
  31.7 2.9 %collective-permute-done.2 = bf16[4,112,256]{2,1,0:T(8,128)(2,1)S(1)} collective-permute-done((bf16[4,112,256]{2,1,0:T(8,128)(2,1)S(1)}, bf16[4,112,256]{2,1,0:T(8,128)(2,1)S(1)}, u32[]{:S(2)}, u32[]{:S(2)}) %collective-permute-start.2) | collective-permute-done | bytes 229408 | tf_op jit(solution)/shard_map/ppermute | solution.py:206
  34.5 11.9 %collective-permute-done.3 = bf16[4,112,256]{2,1,0:T(8,128)(2,1)S(1)} collective-permute-done((bf16[4,112,256]{2,1,0:T(8,128)(2,1)S(1)}, bf16[4,112,256]{2,1,0:T(8,128)(2,1)S(1)}, u32[]{:S(2)}, u32[]{:S(2)}) %collective-permute-start.3) | collective-permute-done | bytes 229408 | tf_op jit(solution)/shard_map/ppermute | solution.py:206
  46.4 0.1 add_convert_fusion.3
  46.5 1.8 %collective-permute-start.11 = (bf16[1,112,256]{2,1,0:T(8,128)(2,1)S(1)}, bf16[1,112,256]{2,1,0:T(8,128)(2,1)S(1)}, u32[]{:S(2)}, u32[]{:S(2)}) collective-permute-start(bf16[1,112,256]{2,1,0:T(8,128)(2,1)S(1)} %get-tuple-element.27), channel_id=1, source_target_pairs={{0,24},{4,28},{8,16},{12,20},{16,8},{20,12},{24,0},{28,4},{1,25},{... | collective-permute-start | bytes 172040 | tf_op jit(solution)/shard_map/ppermute | solution.py:203
  48.3 0.6 collective-permute-start.10
  48.9 0.4 collective-permute-start.9
  49.3 1.3 %collective-permute-done.11.refs_3_ = bf16[1,112,256]{2,1,0:T(8,128)(2,1)S(1)} collective-permute-done((bf16[1,112,256]{2,1,0:T(8,128)(2,1)S(1)}, bf16[1,112,256]{2,1,0:T(8,128)(2,1)S(1)}, u32[]{:S(2)}, u32[]{:S(2)}) %collective-permute-start.11) | collective-permute-done | bytes 57376 | tf_op jit(solution)/shard_map/ppermute | solution.py:203
  50.5 0.8 %collective-permute-done.10.refs_2_ = bf16[1,112,256]{2,1,0:T(8,128)(2,1)S(1)} collective-permute-done((bf16[1,112,256]{2,1,0:T(8,128)(2,1)S(1)}, bf16[1,112,256]{2,1,0:T(8,128)(2,1)S(1)}, u32[]{:S(2)}, u32[]{:S(2)}) %collective-permute-start.10) | collective-permute-done | bytes 57376 | tf_op jit(solution)/shard_map/ppermute | solution.py:203
  51.4 0.6 collective-permute-done.9.refs_1_
  51.9 0.1 turned.1.refs_1_
  52.1 1.3 %collective-permute-start.18 = (bf16[256,256]{1,0:T(8,128)(2,1)S(1)}, bf16[256,256]{1,0:T(8,128)(2,1)S(1)}, u32[]{:S(2)}, u32[]{:S(2)}) collective-permute-start(bf16[256,256]{1,0:T(8,128)(2,1)S(1)} %turned.1.refs_1_), channel_id=1, source_target_pairs={{0,24},{4,28},{8,16},{12,20},{16,8},{20,12},{24,0},{28,4},{1,25},{... | collective-permute-start | bytes 393224 | tf_op jit(solution)/shard_map/ppermute | solution.py:203
  53.3 0.3 collective-permute-start.16
  53.7 1.1 %collective-permute-start.14 = (bf16[256,256]{1,0:T(8,128)(2,1)S(1)}, bf16[256,256]{1,0:T(8,128)(2,1)S(1)}, u32[]{:S(2)}, u32[]{:S(2)}) collective-permute-start(bf16[256,256]{1,0:T(8,128)(2,1)S(1)} %turned.1.refs_1_), channel_id=1, source_target_pairs={{0,16},{4,12},{8,24},{12,4},{16,0},{20,28},{24,8},{28,20},{1,17},{... | collective-permute-start | bytes 393224 | tf_op jit(solution)/shard_map/ppermute | solution.py:203
  54.8 8.0 %collective-permute-start.13 = (bf16[256,256]{1,0:T(8,128)(2,1)S(1)}, bf16[256,256]{1,0:T(8,128)(2,1)S(1)}, u32[]{:S(2)}, u32[]{:S(2)}) collective-permute-start(bf16[256,256]{1,0:T(8,128)(2,1)S(1)} %turned.1.refs_1_), channel_id=1, source_target_pairs={{0,4},{4,0},{8,12},{12,8},{16,20},{20,16},{24,28},{28,24},{1,5},{5... | collective-permute-start | bytes 393224 | tf_op jit(solution)/shard_map/ppermute | solution.py:200
  62.7 0.0 collective-permute-done.18.refs_4_
  62.7 2.4 %collective-permute-start.19 = (bf16[256,256]{1,0:T(8,128)(2,1)S(1)}, bf16[256,256]{1,0:T(8,128)(2,1)S(1)}, u32[]{:S(2)}, u32[]{:S(2)}) collective-permute-start(bf16[256,256]{1,0:T(8,128)(2,1)S(1)} %collective-permute-done.18.refs_4_), channel_id=1, source_target_pairs={{0,4},{4,0},{8,12},{12,8},{16,20},{20,16},{24,28},{28,24},{1,5},{5... | collective-permute-start | bytes 393224 | tf_op jit(solution)/shard_map/ppermute | solution.py:200
  65.1 0.8 %collective-permute-start.17 = (bf16[256,256]{1,0:T(8,128)(2,1)S(1)}, bf16[256,256]{1,0:T(8,128)(2,1)S(1)}, u32[]{:S(2)}, u32[]{:S(2)}) collective-permute-start(bf16[256,256]{1,0:T(8,128)(2,1)S(1)} %collective-permute-done.16.refs_3_), channel_id=1, source_target_pairs={{0,4},{4,0},{8,12},{12,8},{16,20},{20,16},{24,28},{28,24},{1,5},{5... | collective-permute-start | bytes 393224 | tf_op jit(solution)/shard_map/ppermute | solution.py:200
  65.9 0.6 collective-permute-start.15
  66.5 1.0 %update.2.refs_5_ = f32[2048,256]{1,0:T(8,128)} custom-call(f32[2048,256]{1,0:T(8,128)S(1)} %copy-done.1, bf16[256,256]{1,0:T(8,128)(2,1)S(1)} %turned.1.refs_1_, bf16[256,256]{1,0:T(8,128)(2,1)S(1)} %collective-permute-done.14.refs_2_, bf16[256,256]{1,0:T(8,128)(2,1)S(1)} %collective-permute-done.16.refs_3_, ...), custom_call_target="tpu_custom_call" | custom-call | tf_op jit(solution)/shard_map/update/pallas_call | solution.py:139
  67.6 0.0 collective-permute-done.19.refs_4_
  67.6 0.0 collective-permute-done.17.refs_3_
  67.6 1.0 %update.3 = f32[2048,256]{1,0:T(8,128)} custom-call(f32[2048,256]{1,0:T(8,128)S(1)} %copy-done.1, bf16[256,256]{1,0:T(8,128)(2,1)S(1)} %collective-permute-done.13.refs_1_, bf16[256,256]{1,0:T(8,128)(2,1)S(1)} %collective-permute-done.15.refs_2_, bf16[256,256]{1,0:T(8,128)(2,1)S(1)} %collective-permute-done.17.refs_3_, ...), custom_call_target="tpu_custom_call", output_to_operand_aliasing={{}: (5, {})} | custom-call | tf_op jit(solution)/shard_map/update/pallas_call | solution.py:139
  (9 shorter events, 0.1 us)
Async XLA Ops:
  0.0 2.8 %copy-start = (bf16[256,8192]{1,0:T(8,128)(2,1)S(1)}, bf16[256,8192]{1,0:T(8,128)(2,1)}, u32[]{:S(2)}) copy-start(bf16[256,8192]{1,0:T(8,128)(2,1)} %refs_0_.13) | copy-start | bytes 12582916
  2.1 2.4 %collective-permute-start.4 = (bf16[8,144,256]{2,1,0:T(8,128)(2,1)S(1)}, bf16[8,144,256]{2,1,0:T(8,128)(2,1)S(1)}, u32[]{:S(2)}, u32[]{:S(2)}) collective-permute-start(bf16[8,144,256]{2,1,0:T(8,128)(2,1)S(1)} %get-tuple-element.21), channel_id=1, source_target_pairs={{0,4},{4,0},{8,12},{12,8},{16,20},{20,16},{24,28},{28,24},{1,5},{5... | collective-permute-start | bytes 1769480 | tf_op jit(solution)/shard_map/ppermute | solution.py:200
  5.6 2.1 %collective-permute-start.5 = (bf16[8,144,256]{2,1,0:T(8,128)(2,1)S(1)}, bf16[8,144,256]{2,1,0:T(8,128)(2,1)S(1)}, u32[]{:S(2)}, u32[]{:S(2)}) collective-permute-start(bf16[8,144,256]{2,1,0:T(8,128)(2,1)S(1)} %products.10), channel_id=1, source_target_pairs={{0,4},{4,0},{8,12},{12,8},{16,20},{20,16},{24,28},{28,24},{1,5},{5... | collective-permute-start | bytes 1769480 | tf_op jit(solution)/shard_map/ppermute | solution.py:200
  6.1 9.0 %collective-permute-start.6 = (bf16[8,144,256]{2,1,0:T(8,128)(2,1)S(1)}, bf16[8,144,256]{2,1,0:T(8,128)(2,1)S(1)}, u32[]{:S(2)}, u32[]{:S(2)}) collective-permute-start(bf16[8,144,256]{2,1,0:T(8,128)(2,1)S(1)} %products.9), channel_id=1, source_target_pairs={{0,8},{4,20},{8,0},{12,28},{16,24},{20,4},{24,16},{28,12},{1,9},{5... | collective-permute-start | bytes 1769480 | tf_op jit(solution)/shard_map/ppermute | solution.py:203
  7.3 15.2 %collective-permute-start = (bf16[16,112,256]{2,1,0:T(8,128)(2,1)S(1)}, bf16[16,112,256]{2,1,0:T(8,128)(2,1)S(1)}, u32[]{:S(2)}, u32[]{:S(2)}) collective-permute-start(bf16[16,112,256]{2,1,0:T(8,128)(2,1)S(1)} %products.7), channel_id=1, source_target_pairs={{0,4},{4,0},{8,12},{12,8},{16,20},{20,16},{24,28},{28,24},{1,5},{5... | collective-permute-start | bytes 2752520 | tf_op jit(solution)/shard_map/ppermute | solution.py:200
  15.2 5.9 %collective-permute-start.7 = (bf16[4,144,256]{2,1,0:T(8,128)(2,1)S(1)}, bf16[4,144,256]{2,1,0:T(8,128)(2,1)S(1)}, u32[]{:S(2)}, u32[]{:S(2)}) collective-permute-start(bf16[4,144,256]{2,1,0:T(8,128)(2,1)S(1)} %add_convert_fusion), channel_id=1, source_target_pairs={{0,16},{4,12},{8,24},{12,4},{16,0},{20,28},{24,8},{28,20},{1,17},{... | collective-permute-start | bytes 884744 | tf_op jit(solution)/shard_map/ppermute | solution.py:203
  21.2 5.1 %collective-permute-start.8 = (bf16[2,144,256]{2,1,0:T(8,128)(2,1)S(1)}, bf16[2,144,256]{2,1,0:T(8,128)(2,1)S(1)}, u32[]{:S(2)}, u32[]{:S(2)}) collective-permute-start(bf16[2,144,256]{2,1,0:T(8,128)(2,1)S(1)} %add_convert_fusion.1), channel_id=1, source_target_pairs={{0,1},{1,0},{2,3},{3,2},{4,5},{5,4},{6,7},{7,6},{8,9},{9,8},{10,11... | collective-permute-start | bytes 442376 | tf_op jit(solution)/shard_map/ppermute | solution.py:206
  23.6 43.0 %copy-start.1 = (f32[2048,256]{1,0:T(8,128)S(1)}, f32[2048,256]{1,0:T(8,128)}, u32[]{:S(2)}) copy-start(f32[2048,256]{1,0:T(8,128)} %refs_0_.15) | copy-start | bytes 6291460
  23.6 8.1 %collective-permute-start.1 = (bf16[4,112,256]{2,1,0:T(8,128)(2,1)S(1)}, bf16[4,112,256]{2,1,0:T(8,128)(2,1)S(1)}, u32[]{:S(2)}, u32[]{:S(2)}) collective-permute-start(bf16[4,112,256]{2,1,0:T(8,128)(2,1)S(1)} %get-tuple-element.18), channel_id=1, source_target_pairs={{0,1},{1,0},{2,3},{3,2},{4,5},{5,4},{6,7},{7,6},{8,9},{9,8},{10,11... | collective-permute-start | bytes 688136 | tf_op jit(solution)/shard_map/ppermute | solution.py:206
  23.8 10.7 %collective-permute-start.2 = (bf16[4,112,256]{2,1,0:T(8,128)(2,1)S(1)}, bf16[4,112,256]{2,1,0:T(8,128)(2,1)S(1)}, u32[]{:S(2)}, u32[]{:S(2)}) collective-permute-start(bf16[4,112,256]{2,1,0:T(8,128)(2,1)S(1)} %get-tuple-element.19), channel_id=1, source_target_pairs={{0,2},{1,3},{2,0},{3,1},{4,6},{5,7},{6,4},{7,5},{8,10},{9,11},{10,... | collective-permute-start | bytes 688136 | tf_op jit(solution)/shard_map/ppermute | solution.py:206
  23.8 22.6 %collective-permute-start.3 = (bf16[4,112,256]{2,1,0:T(8,128)(2,1)S(1)}, bf16[4,112,256]{2,1,0:T(8,128)(2,1)S(1)}, u32[]{:S(2)}, u32[]{:S(2)}) collective-permute-start(bf16[4,112,256]{2,1,0:T(8,128)(2,1)S(1)} %get-tuple-element.20), channel_id=1, source_target_pairs={{0,3},{1,2},{2,1},{3,0},{4,7},{5,6},{6,5},{7,4},{8,11},{9,10},{10,... | collective-permute-start | bytes 688136 | tf_op jit(solution)/shard_map/ppermute | solution.py:206
  26.3 25.6 %collective-permute-start.12 = (bf16[1,144,256]{2,1,0:T(8,128)(2,1)S(1)}, bf16[1,144,256]{2,1,0:T(8,128)(2,1)S(1)}, u32[]{:S(2)}, u32[]{:S(2)}) collective-permute-start(bf16[1,144,256]{2,1,0:T(8,128)(2,1)S(1)} %add_convert_fusion.2), channel_id=1, source_target_pairs={{0,2},{1,3},{2,0},{3,1},{4,6},{5,7},{6,4},{7,5},{8,10},{9,11},{10,... | collective-permute-start | bytes 221192 | tf_op jit(solution)/shard_map/ppermute | solution.py:206
  46.5 4.0 %collective-permute-start.11 = (bf16[1,112,256]{2,1,0:T(8,128)(2,1)S(1)}, bf16[1,112,256]{2,1,0:T(8,128)(2,1)S(1)}, u32[]{:S(2)}, u32[]{:S(2)}) collective-permute-start(bf16[1,112,256]{2,1,0:T(8,128)(2,1)S(1)} %get-tuple-element.27), channel_id=1, source_target_pairs={{0,24},{4,28},{8,16},{12,20},{16,8},{20,12},{24,0},{28,4},{1,25},{... | collective-permute-start | bytes 172040 | tf_op jit(solution)/shard_map/ppermute | solution.py:203
  48.3 3.0 %collective-permute-start.10 = (bf16[1,112,256]{2,1,0:T(8,128)(2,1)S(1)}, bf16[1,112,256]{2,1,0:T(8,128)(2,1)S(1)}, u32[]{:S(2)}, u32[]{:S(2)}) collective-permute-start(bf16[1,112,256]{2,1,0:T(8,128)(2,1)S(1)} %get-tuple-element.28), channel_id=1, source_target_pairs={{0,8},{4,20},{8,0},{12,28},{16,24},{20,4},{24,16},{28,12},{1,9},{5... | collective-permute-start | bytes 172040 | tf_op jit(solution)/shard_map/ppermute | solution.py:203
  48.9 3.0 %collective-permute-start.9 = (bf16[1,112,256]{2,1,0:T(8,128)(2,1)S(1)}, bf16[1,112,256]{2,1,0:T(8,128)(2,1)S(1)}, u32[]{:S(2)}, u32[]{:S(2)}) collective-permute-start(bf16[1,112,256]{2,1,0:T(8,128)(2,1)S(1)} %get-tuple-element.29), channel_id=1, source_target_pairs={{0,16},{4,12},{8,24},{12,4},{16,0},{20,28},{24,8},{28,20},{1,17},{... | collective-permute-start | bytes 172040 | tf_op jit(solution)/shard_map/ppermute | solution.py:203
  52.1 10.7 %collective-permute-start.18 = (bf16[256,256]{1,0:T(8,128)(2,1)S(1)}, bf16[256,256]{1,0:T(8,128)(2,1)S(1)}, u32[]{:S(2)}, u32[]{:S(2)}) collective-permute-start(bf16[256,256]{1,0:T(8,128)(2,1)S(1)} %turned.1.refs_1_), channel_id=1, source_target_pairs={{0,24},{4,28},{8,16},{12,20},{16,8},{20,12},{24,0},{28,4},{1,25},{... | collective-permute-start | bytes 393224 | tf_op jit(solution)/shard_map/ppermute | solution.py:203
  53.3 11.8 %collective-permute-start.16 = (bf16[256,256]{1,0:T(8,128)(2,1)S(1)}, bf16[256,256]{1,0:T(8,128)(2,1)S(1)}, u32[]{:S(2)}, u32[]{:S(2)}) collective-permute-start(bf16[256,256]{1,0:T(8,128)(2,1)S(1)} %turned.1.refs_1_), channel_id=1, source_target_pairs={{0,8},{4,20},{8,0},{12,28},{16,24},{20,4},{24,16},{28,12},{1,9},{5... | collective-permute-start | bytes 393224 | tf_op jit(solution)/shard_map/ppermute | solution.py:203
  53.7 12.2 %collective-permute-start.14 = (bf16[256,256]{1,0:T(8,128)(2,1)S(1)}, bf16[256,256]{1,0:T(8,128)(2,1)S(1)}, u32[]{:S(2)}, u32[]{:S(2)}) collective-permute-start(bf16[256,256]{1,0:T(8,128)(2,1)S(1)} %turned.1.refs_1_), channel_id=1, source_target_pairs={{0,16},{4,12},{8,24},{12,4},{16,0},{20,28},{24,8},{28,20},{1,17},{... | collective-permute-start | bytes 393224 | tf_op jit(solution)/shard_map/ppermute | solution.py:203
  54.8 12.8 %collective-permute-start.13 = (bf16[256,256]{1,0:T(8,128)(2,1)S(1)}, bf16[256,256]{1,0:T(8,128)(2,1)S(1)}, u32[]{:S(2)}, u32[]{:S(2)}) collective-permute-start(bf16[256,256]{1,0:T(8,128)(2,1)S(1)} %turned.1.refs_1_), channel_id=1, source_target_pairs={{0,4},{4,0},{8,12},{12,8},{16,20},{20,16},{24,28},{28,24},{1,5},{5... | collective-permute-start | bytes 393224 | tf_op jit(solution)/shard_map/ppermute | solution.py:200
  62.7 4.8 %collective-permute-start.19 = (bf16[256,256]{1,0:T(8,128)(2,1)S(1)}, bf16[256,256]{1,0:T(8,128)(2,1)S(1)}, u32[]{:S(2)}, u32[]{:S(2)}) collective-permute-start(bf16[256,256]{1,0:T(8,128)(2,1)S(1)} %collective-permute-done.18.refs_4_), channel_id=1, source_target_pairs={{0,4},{4,0},{8,12},{12,8},{16,20},{20,16},{24,28},{28,24},{1,5},{5... | collective-permute-start | bytes 393224 | tf_op jit(solution)/shard_map/ppermute | solution.py:200
  65.1 2.5 %collective-permute-start.17 = (bf16[256,256]{1,0:T(8,128)(2,1)S(1)}, bf16[256,256]{1,0:T(8,128)(2,1)S(1)}, u32[]{:S(2)}, u32[]{:S(2)}) collective-permute-start(bf16[256,256]{1,0:T(8,128)(2,1)S(1)} %collective-permute-done.16.refs_3_), channel_id=1, source_target_pairs={{0,4},{4,0},{8,12},{12,8},{16,20},{20,16},{24,28},{28,24},{1,5},{5... | collective-permute-start | bytes 393224 | tf_op jit(solution)/shard_map/ppermute | solution.py:200
  65.9 1.7 %collective-permute-start.15 = (bf16[256,256]{1,0:T(8,128)(2,1)S(1)}, bf16[256,256]{1,0:T(8,128)(2,1)S(1)}, u32[]{:S(2)}, u32[]{:S(2)}) collective-permute-start(bf16[256,256]{1,0:T(8,128)(2,1)S(1)} %collective-permute-done.14.refs_2_), channel_id=1, source_target_pairs={{0,4},{4,0},{8,12},{12,8},{16,20},{20,16},{24,28},{28,24},{1,5},{5... | collective-permute-start | bytes 393224 | tf_op jit(solution)/shard_map/ppermute | solution.py:200
